TPU v7x, 32 devices: a whole 2x2x4 slice. The times are simulated.
32 devices in a mesh: boxes: 32 (over z, y, x, core).
Axes of the slice: x: 2, y: 2, z: 4, core: 2. Of those that a mesh axis runs over, the one named last changes fastest.
Arguments:
- random_block: bfloat16 [512, 256, 128], P('boxes'), may hold values from -6 to 6
- sample_block: bfloat16 [512, 256, 128], P('boxes'), may hold values from -12 to 12
- near_blocks: bfloat16 [512, 8, 256, 256], P('boxes'), may hold values from -0.375 to 0.375
- near_index: int32 [512, 8], P('boxes'), may hold values from 0 to 511, as said below
- near_count: int32 [512], P('boxes'), may hold values from 2 to 8
Outputs:
- leaf_sketch: bfloat16 [512, 256, 128], P('boxes')
- level_sketch: bfloat16 [32, 9, 128, 128], P('boxes')
Inputs may be any that keep to these rules, and one draw needn't show every extreme that they name: near_index[b, 0] = b; every entry lies within 16 boxes of b; entries at slots from near_count[b] on are ignored.
All inputs are finite; a program needn't handle non-finite values.
Results may differ from a plain program's by a relative error of at most 0.001.
Values may be sent and summed in bfloat16 or wider, within the bound.
A program may use at most 192 MiB of HBM per device.

v0:
```python
import functools

import jax
import jax.numpy as jnp
from jax import lax
from jax.experimental import pallas as pl
from jax.experimental.pallas import tpu as pltpu
from jax.sharding import PartitionSpec as P

exact_mode = lax.Precision.HIGHEST


def exact_dot(a, b):
    return jnp.dot(a, b, precision=exact_mode, preferred_element_type=jnp.float32)


def gram_kernel(ids, counts, blocks, sample, low, own, high, grams, compact, wide, sems):
    box = pl.program_id(0)
    count = own.shape[0]
    slots, samples = blocks.shape[1], sample.shape[2]
    half = samples // 2

    @pl.when(box == 0)
    def _():
        copies = [
            pltpu.make_async_copy(part, wide.at[pl.ds(place * count, count)], sems.at[place])
            for place, part in enumerate((low, own, high))
        ]
        for copy in copies:
            copy.start()
        for copy in copies:
            copy.wait()

    for part in range(blocks.shape[0]):
        here = box * blocks.shape[0] + part
        total = jnp.zeros(sample.shape[1:], jnp.float32)
        for slot in range(slots):
            keep = (slot < counts[here]).astype(jnp.float32).astype(jnp.bfloat16)
            picked = wide[ids[here * slots + slot]] * keep
            total += jnp.dot(blocks[part, slot], picked, preferred_element_type=jnp.float32)
        far = sample[part].astype(jnp.float32) - total
        doubled = far + pltpu.roll(far, half, 1)
        compact[part] = doubled
        random = wide[count + here].astype(jnp.float32)
        flipped = doubled.T[:half]
        grams[part] = exact_dot(flipped, jnp.concatenate([doubled, random], axis=1))


def gram_call(ids, counts, blocks, sample, low, own, high):
    count, rows, samples = sample.shape
    slots = blocks.shape[1]
    half = samples // 2
    together = 4 if count % 4 == 0 else 1
    anywhere = pl.BlockSpec(memory_space=pl.ANY)
    return pl.pallas_call(
        gram_kernel,
        grid_spec=pltpu.PrefetchScalarGridSpec(
            num_scalar_prefetch=2,
            grid=(count // together,),
            in_specs=[
                pl.BlockSpec((together, slots, rows, rows), lambda b, *_: (b, 0, 0, 0)),
                pl.BlockSpec((together, rows, samples), lambda b, *_: (b, 0, 0)),
                anywhere,
                anywhere,
                anywhere,
            ],
            out_specs=[
                pl.BlockSpec((together, half, 2 * samples), lambda b, *_: (b, 0, 0)),
                pl.BlockSpec((together, rows, samples), lambda b, *_: (b, 0, 0)),
            ],
            scratch_shapes=[
                pltpu.VMEM((3 * count, rows, samples), jnp.bfloat16),
                pltpu.SemaphoreType.DMA((3,)),
            ],
        ),
        out_shape=[
            jax.ShapeDtypeStruct((count, half, 2 * samples), jnp.float32),
            jax.ShapeDtypeStruct((count, rows, samples), jnp.float32),
        ],
        name="gram",
    )(ids, counts, blocks, sample, low, own, high)


def eliminate(nodes, low_k, high_k, half, work, uppers, with_upper):
    samples = 2 * half
    lanes = lax.broadcasted_iota(jnp.int32, (1, samples), 1)

    rows = lax.broadcasted_iota(jnp.int32, (half, samples), 0)
    group = 4

    def step(k, carry):
        at_k = lanes == k
        kept = (lanes >= k) & (lanes < half)
        row_k = rows == k
        pivots = {node: work[node, pl.ds(k, 1), :] for node in nodes}
        picked = {
            node: jnp.sum(jnp.where(at_k, pivots[node], 0.0), axis=1, keepdims=True)
            for node in nodes
        }
        scaled = {node: pivots[node] / picked[node] for node in nodes}
        for node, place in with_upper.items():
            uppers[place, pl.ds(k, 1), :] = jnp.where(
                kept, pivots[node] * lax.rsqrt(picked[node]), 0.0
            )
        for first in range(0, len(nodes), group):
            members = nodes[first : first + group]
            matrices = [work[node] for node in members]
            columns = [
                jnp.sum(jnp.where(at_k, matrix, 0.0), axis=1, keepdims=True)
                for matrix in matrices
            ]
            for node, matrix, column in zip(members, matrices, columns):
                work[node] = jnp.where(row_k, scaled[node], matrix - column * scaled[node])
        return carry

    lax.fori_loop(low_k, high_k, step, 0)


def start_matrix(gram, half):
    samples = 2 * half
    rows = lax.broadcasted_iota(jnp.int32, (half, samples), 0)
    lanes = lax.broadcasted_iota(jnp.int32, (half, samples), 1)
    return jnp.where(lanes < half, gram, (lanes - half == rows).astype(jnp.float32))


def solved(work, node, moment):
    blank = jnp.zeros_like(moment)
    answer = exact_dot(work[node], jnp.concatenate([blank, moment], axis=0))
    return jnp.concatenate([answer, blank], axis=0)


def tree_kernel(
    spread, grams, compact, leaf_out, level_out, work, moments, uppers, sums, arrived, sent, landed
):
    count = grams.shape[0]
    half, samples = grams.shape[1], grams.shape[2] // 2
    depth = count.bit_length() - 1
    me = lax.axis_index("boxes")
    bits = [lax.rem(lax.div(me, 1 << step), 2) for step in range(spread)]
    partners = [me + (1 - 2 * bit) * (1 << step) for step, bit in enumerate(bits)]
    barrier = pltpu.get_barrier_semaphore()
    for partner in partners:
        pl.semaphore_signal(
            barrier, inc=1, device_id=(partner,), device_id_type=pl.DeviceIdType.MESH
        )
    summed = grams[0]
    for leaf in range(1, count):
        summed = summed + grams[leaf]
    sums[0] = summed

    def exchange(step):
        return pltpu.make_async_remote_copy(
            src_ref=sums.at[step],
            dst_ref=arrived.at[step],
            send_sem=sent.at[step],
            recv_sem=landed.at[step],
            device_id=(partners[step],),
            device_id_type=pl.DeviceIdType.MESH,
        )

    pl.semaphore_wait(barrier, spread)
    copies = [exchange(step) for step in range(spread)]
    copies[0].start()
    for node in range(count):
        work[node] = start_matrix(grams[node, :, :samples], half)
    place = 0
    for height in range(1, depth + 1):
        for side in range(1 if height == depth else 2):
            first = side * 2**height
            part = grams[first]
            for leaf in range(first + 1, first + 2**height):
                part = part + grams[leaf]
            work[count + place] = start_matrix(part[:, :samples], half)
            moments[place] = part[:, samples:]
            place += 1
    below = count + place
    with_upper = {0: 0, 1: 1}
    for node in range(place):
        with_upper[count + node] = 2 + node
    own = 1 + place
    nodes = list(range(below))
    for step in range(spread):
        eliminate(
            nodes, half * step // spread, half * (step + 1) // spread, half, work, uppers, with_upper
        )
        copies[step].wait()
        sums[step + 1] = sums[step] + arrived[step]
        if step + 1 < spread:
            copies[step + 1].start()
    for step in range(spread):
        work[below + 2 * step] = start_matrix(arrived[step, :, :samples], half)
        work[below + 2 * step + 1] = start_matrix(sums[step + 1, :, :samples], half)
    nodes = list(range(below, below + 2 * spread))
    later = {node: own + 1 + node - below for node in nodes[:-1]}
    eliminate(nodes, 0, half, half, work, uppers, later)
    for leaf in range(count):
        answer = solved(work, leaf, grams[leaf, :, samples:])
        leaf_out[leaf] = exact_dot(compact[leaf], answer).astype(leaf_out.dtype)
    for height in range(1, depth + 1):
        place = 2 * (height - 1)
        answer = solved(work, count + place, moments[place])
        stacked = jnp.concatenate([uppers[place], uppers[place + 1]], axis=0)
        level_out[0, height - 1] = exact_dot(stacked, answer).astype(level_out.dtype)
    for step in range(spread):
        mine, other = uppers[own + 2 * step], uppers[own + 2 * step + 1]
        odd = bits[step] == 1
        stacked = jnp.concatenate(
            [jnp.where(odd, other, mine), jnp.where(odd, mine, other)], axis=0
        )
        answer = solved(work, below + 2 * step + 1, sums[step + 1, :, samples:])
        level_out[0, depth + step] = exact_dot(stacked, answer).astype(level_out.dtype)


def tree_call(grams, compact, spread):
    count, half, double = grams.shape
    samples = double // 2
    depth = count.bit_length() - 1
    extra = 2 * depth - 1
    return pl.pallas_call(
        functools.partial(tree_kernel, spread),
        in_specs=[pl.BlockSpec(memory_space=pltpu.VMEM)] * 2,
        out_specs=[pl.BlockSpec(memory_space=pltpu.VMEM)] * 2,
        out_shape=[
            jax.ShapeDtypeStruct(compact.shape, jnp.bfloat16),
            jax.ShapeDtypeStruct((1, depth + spread, samples, samples), jnp.bfloat16),
        ],
        scratch_shapes=[
            pltpu.VMEM((count + extra + 2 * spread, half, samples), jnp.float32),
            pltpu.VMEM((extra, half, samples), jnp.float32),
            pltpu.VMEM((2 + extra + 2 * spread - 1, half, samples), jnp.float32),
            pltpu.VMEM((spread + 1, half, double), jnp.float32),
            pltpu.VMEM((spread, half, double), jnp.float32),
            pltpu.SemaphoreType.DMA((spread,)),
            pltpu.SemaphoreType.DMA((spread,)),
        ],
        compiler_params=pltpu.CompilerParams(collective_id=0, has_side_effects=True),
        name="tree",
    )(grams, compact)


def per_device(random_block, sample_block, near_blocks, near_index, near_count):
    count = random_block.shape[0]
    device = lax.axis_index("boxes")
    size = lax.axis_size("boxes")
    forward = [(i, i + 1) for i in range(size - 1)]
    backward = [(target, source) for source, target in forward]
    low = lax.ppermute(random_block, "boxes", forward)
    high = lax.ppermute(random_block, "boxes", backward)
    ids = jnp.clip(near_index - device * count + count, 0, 3 * count - 1).reshape(-1)
    grams, compact = gram_call(
        ids, near_count, near_blocks, sample_block, low, random_block, high
    )
    return tuple(tree_call(grams, compact, size.bit_length() - 1))


def solution(mesh):
    return jax.shard_map(
        per_device,
        mesh=mesh,
        in_specs=(
            P("boxes", None, None),
            P("boxes", None, None),
            P("boxes", None, None, None),
            P("boxes", None),
            P("boxes"),
        ),
        out_specs=(P("boxes", None, None), P("boxes", None, None, None)),
        check_vma=False,
    )
```

profile of v0, /device:TPU:0, one launch (start us, length us, event | category | flops | bytes accessed | tf_op | source)
XLA Modules:
  0.0 95.1 jit_solution(18241788667830198531)
XLA Ops:
  0.6 2.5 %collective-permute-start = (bf16[16,256,128]{2,1,0:T(8,128)(2,1)}, bf16[16,256,128]{2,1,0:T(8,128)(2,1)S(1)}, u32[]{:S(2)}, u32[]{:S(2)}) collective-permute-start(bf16[16,256,128]{2,1,0:T(8,128)(2,1)} %own.1), channel_id=1, source_target_pairs={{0,1},{1,2},{2,3},{3,4},{4,5},{5,6},{6,7},{7,8},{8,9},{9,10},{10,1... | collective-permute-start | bytes 3145736 | tf_op jit(solution)/shard_map/ppermute | solution.py:247
  3.1 1.3 %collective-permute-start.1 = (bf16[16,256,128]{2,1,0:T(8,128)(2,1)}, bf16[16,256,128]{2,1,0:T(8,128)(2,1)S(1)}, u32[]{:S(2)}, u32[]{:S(2)}) collective-permute-start(bf16[16,256,128]{2,1,0:T(8,128)(2,1)} %own.1), channel_id=1, source_target_pairs={{1,0},{2,1},{3,2},{4,3},{5,4},{6,5},{7,6},{8,7},{9,8},{10,9},{11,1... | collective-permute-start | bytes 3145736 | tf_op jit(solution)/shard_map/ppermute | solution.py:248
  4.4 0.7 add_clamp_fusion
  5.1 0.1 copy.8
  5.2 0.6 reshape.7.ids
  5.8 0.0 collective-permute-done.low
  5.8 0.0 copy-start
  5.8 4.1 %collective-permute-done.1.high = bf16[16,256,128]{2,1,0:T(8,128)(2,1)S(1)} collective-permute-done((bf16[16,256,128]{2,1,0:T(8,128)(2,1)}, bf16[16,256,128]{2,1,0:T(8,128)(2,1)S(1)}, u32[]{:S(2)}, u32[]{:S(2)}) %collective-permute-start.1) | collective-permute-done | bytes 1048608 | tf_op jit(solution)/shard_map/ppermute | solution.py:248
  9.9 0.0 copy-done
  9.9 0.0 copy-start.1
  9.9 1.0 %copy-done.1 = bf16[16,256,128]{2,1,0:T(8,128)(2,1)} copy-done((bf16[16,256,128]{2,1,0:T(8,128)(2,1)}, bf16[16,256,128]{2,1,0:T(8,128)(2,1)S(1)}, u32[]{:S(2)}) %copy-start.1) | copy-done | bytes 1048600
  10.9 17.5 %gram.1 = (f32[16,64,256]{2,1,0:T(8,128)}, f32[16,256,128]{2,1,0:T(8,128)}) custom-call(s32[128]{0:T(128)} %reshape.7.ids, s32[16]{0:T(128)} %counts.1, bf16[16,8,256,256]{3,2,1,0:T(8,128)(2,1)} %blocks.1, bf16[16,256,128]{2,1,0:T(8,128)(2,1)} %sample.1, bf16[16,256,128]{2,1,0:T(8,128)(2,1)} %copy-done, bf16[16,256,128]{2,1,0:T(8,128)(2,1)} %own.1, ...), custom_call_target="tpu_custom_call" | custom-call | tf_op jit(solution)/shard_map/gram/pallas_call | solution.py:55
  28.3 62.8 %tree.1 = (bf16[16,256,128]{2,1,0:T(8,128)(2,1)}, bf16[1,9,128,128]{3,2,1,0:T(8,128)(2,1)}) custom-call(f32[16,64,256]{2,1,0:T(8,128)} %get-tuple-element.4.grams, f32[16,256,128]{2,1,0:T(8,128)} %get-tuple-element.5.compact), custom_call_target="tpu_custom_call" | custom-call | tf_op jit(solution)/shard_map/tree/pallas_call | solution.py:219
  91.1 2.3 %copy.11 = bf16[16,256,128]{2,1,0:T(8,128)(2,1)} copy(bf16[16,256,128]{2,1,0:T(8,128)(2,1)} %get-tuple-element.8) | data formatting | bytes 2097152
  93.4 1.7 %copy.12 = bf16[1,9,128,128]{3,2,1,0:T(8,128)(2,1)} copy(bf16[1,9,128,128]{3,2,1,0:T(8,128)(2,1)} %get-tuple-element.9) | data formatting | bytes 589824
Async XLA Ops:
  0.6 5.2 %collective-permute-start = (bf16[16,256,128]{2,1,0:T(8,128)(2,1)}, bf16[16,256,128]{2,1,0:T(8,128)(2,1)S(1)}, u32[]{:S(2)}, u32[]{:S(2)}) collective-permute-start(bf16[16,256,128]{2,1,0:T(8,128)(2,1)} %own.1), channel_id=1, source_target_pairs={{0,1},{1,2},{2,3},{3,4},{4,5},{5,6},{6,7},{7,8},{8,9},{9,10},{10,1... | collective-permute-start | bytes 3145736 | tf_op jit(solution)/shard_map/ppermute | solution.py:247
  3.1 6.8 %collective-permute-start.1 = (bf16[16,256,128]{2,1,0:T(8,128)(2,1)}, bf16[16,256,128]{2,1,0:T(8,128)(2,1)S(1)}, u32[]{:S(2)}, u32[]{:S(2)}) collective-permute-start(bf16[16,256,128]{2,1,0:T(8,128)(2,1)} %own.1), channel_id=1, source_target_pairs={{1,0},{2,1},{3,2},{4,3},{5,4},{6,5},{7,6},{8,7},{9,8},{10,9},{11,1... | collective-permute-start | bytes 3145736 | tf_op jit(solution)/shard_map/ppermute | solution.py:248
  5.8 4.1 %copy-start = (bf16[16,256,128]{2,1,0:T(8,128)(2,1)}, bf16[16,256,128]{2,1,0:T(8,128)(2,1)S(1)}, u32[]{:S(2)}) copy-start(bf16[16,256,128]{2,1,0:T(8,128)(2,1)S(1)} %collective-permute-done.low) | copy-start | bytes 3145732
  9.9 1.0 %copy-start.1 = (bf16[16,256,128]{2,1,0:T(8,128)(2,1)}, bf16[16,256,128]{2,1,0:T(8,128)(2,1)S(1)}, u32[]{:S(2)}) copy-start(bf16[16,256,128]{2,1,0:T(8,128)(2,1)S(1)} %collective-permute-done.1.high) | copy-start | bytes 3145732
where the time goes:
time: 95.4 us; the launch traced here: 95.1 us
  Pallas kernels  80.2 us (84%)
  local copies, waits for them, and re-layouts  5.65 us (6%)
  waiting for transfers between devices  4.12 us (4%)
  starting transfers between devices  3.76 us (4%)
    pallas_call x1, Pallas kernels, tree_call(): pl.pallas_call(functools.partial(tree_kernel, spread), in_specs=[pl.Block...  62.8 us
    pallas_call x1, Pallas kernels, gram_call(): pl.pallas_call(gram_kernel, grid_spec=pltpu.PrefetchScalarGridSpec(num_sc...  17.5 us
    unnamed x6, local copies, waits for them, and re-layouts  4.97 us
    ppermute x1, waiting for transfers between devices, per_device(): high = lax.ppermute(random_block, 'boxes', backward)  4.11 us
    ppermute x1, starting transfers between devices, per_device(): low = lax.ppermute(random_block, 'boxes', forward)  2.47 us
  transfers between devices with their start and end apart: 2, of which 1 were waited for; matrix products, arithmetic and copies ran while one was open for 1% of the time, Pallas kernels for 0%

commit v1 on v0

v1 whole, which is shorter than its diff:
```python
import functools

import jax
import jax.numpy as jnp
from jax import lax
from jax.experimental import pallas as pl
from jax.experimental.pallas import tpu as pltpu
from jax.sharding import PartitionSpec as P

AXIS = "boxes"
MESH = pl.DeviceIdType.MESH


def fine_dot(a, b, dims=((1,), (0,))):
    return lax.dot_general(
        a, b, (dims, ((), ())), precision=lax.Precision.HIGH, preferred_element_type=jnp.float32
    )


def halo_kernel(index, counts, source, blocks, sample, part, halo, wide, copy_sem, sent, landed):
    box = pl.program_id(0)
    count = source.shape[0]
    slots, samples = blocks.shape[1], sample.shape[2]
    size = lax.axis_size(AXIS)
    me = lax.axis_index(AXIS)
    core = lax.rem(me, 2)
    partner = me + 1 - 2 * core
    across = me - 1 + 2 * core
    inside = (across >= 0) & (across < size)

    def local_copy():
        return pltpu.make_async_copy(source, wide.at[pl.ds(0, count)], copy_sem)

    def near_copy():
        return pltpu.make_async_remote_copy(
            src_ref=source,
            dst_ref=wide.at[pl.ds(count, count)],
            send_sem=sent.at[0],
            recv_sem=landed.at[0],
            device_id=(partner,),
            device_id_type=MESH,
        )

    def far_copy():
        return pltpu.make_async_remote_copy(
            src_ref=source,
            dst_ref=halo,
            send_sem=sent.at[1],
            recv_sem=landed.at[1],
            device_id=(across,),
            device_id_type=MESH,
        )

    @pl.when(box == 0)
    def _():
        local_copy().start()
        barrier = pltpu.get_barrier_semaphore()
        pl.semaphore_signal(barrier, inc=1, device_id=(partner,), device_id_type=MESH)

        @pl.when(inside)
        def _():
            pl.semaphore_signal(barrier, inc=1, device_id=(across,), device_id_type=MESH)
            pl.semaphore_wait(barrier, 2)
            far_copy().start()

        @pl.when(jnp.logical_not(inside))
        def _():
            pl.semaphore_wait(barrier, 1)

        near_copy().start()
        local_copy().wait()
        near_copy().wait()

    total = jnp.zeros(sample.shape[1:], jnp.float32)
    for slot in range(slots):
        place = index[box, slot] - me * count
        other = place - (1 - 2 * core) * count
        own = (place >= 0) & (place < count)
        beside = (other >= 0) & (other < count)
        pick = jnp.where(own, place, jnp.where(beside, other + count, 0))
        keep = ((own | beside) & (slot < counts[box])).astype(jnp.float32).astype(jnp.bfloat16)
        total += jnp.dot(blocks[0, slot], wide[pick] * keep, preferred_element_type=jnp.float32)
    part[0] = sample[0].astype(jnp.float32) - total

    @pl.when((box == pl.num_programs(0) - 1) & inside)
    def _():
        far_copy().wait()


def halo_call(index, counts, source, blocks, sample):
    count, rows, samples = sample.shape
    slots = blocks.shape[1]
    anywhere = pl.BlockSpec(memory_space=pl.ANY)
    return pl.pallas_call(
        halo_kernel,
        grid_spec=pltpu.PrefetchScalarGridSpec(
            num_scalar_prefetch=0,
            grid=(count,),
            in_specs=[
                pl.BlockSpec(memory_space=pltpu.SMEM),
                pl.BlockSpec(memory_space=pltpu.SMEM),
                anywhere,
                pl.BlockSpec((1, slots, rows, rows), lambda b: (b, 0, 0, 0)),
                pl.BlockSpec((1, rows, samples), lambda b: (b, 0, 0)),
            ],
            out_specs=[pl.BlockSpec((1, rows, samples), lambda b: (b, 0, 0)), anywhere],
            scratch_shapes=[
                pltpu.VMEM((2 * count, rows, samples), jnp.bfloat16),
                pltpu.SemaphoreType.DMA,
                pltpu.SemaphoreType.DMA((2,)),
                pltpu.SemaphoreType.DMA((2,)),
            ],
        ),
        out_shape=[
            jax.ShapeDtypeStruct(sample.shape, jnp.float32),
            jax.ShapeDtypeStruct(sample.shape, jnp.bfloat16),
        ],
        compiler_params=pltpu.CompilerParams(collective_id=0, has_side_effects=True),
        name="halo",
    )(index, counts, source, blocks, sample)


def split_three(value):
    high = value.astype(jnp.bfloat16)
    rest = value - high.astype(jnp.float32)
    middle = rest.astype(jnp.bfloat16)
    low = (rest - middle.astype(jnp.float32)).astype(jnp.bfloat16)
    return high, middle, low


def gram_kernel(index, counts, part, source, halo, blocks, start, moment, compact, held, far, sems):
    step = pl.program_id(0)
    steps = pl.num_programs(0)
    together, rows, samples = part.shape
    count = halo.shape[0]
    slots = held.shape[1]
    half = samples // 2
    me = lax.axis_index(AXIS)
    core = lax.rem(me, 2)
    base = (me - 1 + 2 * core) * count

    def wanted(box, slot):
        place = index[box, slot] - base
        return place, (place >= 0) & (place < count) & (slot < counts[box])

    def fetch(box, slot):
        return pltpu.make_async_copy(blocks.at[box, slot], held.at[box, slot], sems.at[box])

    def issue(which):
        for member in range(together):
            box = which * together + member
            for slot in range(1, slots):
                place, needed = wanted(box, slot)

                @pl.when(needed)
                def _():
                    fetch(box, slot).start()

    @pl.when(step == 0)
    def _():
        issue(0)

    @pl.when(step + 1 < steps)
    def _():
        issue(step + 1)

    for member in range(together):
        box = step * together + member
        far[member] = part[member]
        for slot in range(1, slots):
            place, needed = wanted(box, slot)

            @pl.when(needed)
            def _():
                fetch(box, slot).wait()

        for slot in range(1, slots):
            place, needed = wanted(box, slot)

            @pl.when(needed)
            def _():
                far[member] -= jnp.dot(
                    held[box, slot], halo[place], preferred_element_type=jnp.float32
                )

    lanes_rows = lax.broadcasted_iota(jnp.int32, (rows, samples), 1)
    lanes = lax.broadcasted_iota(jnp.int32, (half, samples), 1)
    diagonal = lanes - half == lax.broadcasted_iota(jnp.int32, (half, samples), 0)
    for member in range(together):
        value = far[member]
        doubled = value + pltpu.roll(value, half, 1)
        flipped = doubled.T[:half]
        high, middle, low = split_three(flipped)
        left = jnp.concatenate([high, middle, low], axis=0)
        top = doubled.astype(jnp.bfloat16)
        next_top = doubled - top.astype(jnp.float32)
        both = jnp.where(lanes_rows < half, top.astype(jnp.float32), next_top).astype(jnp.bfloat16)
        compact[member] = both
        product = jnp.dot(
            left,
            jnp.concatenate([source[member], both], axis=1),
            preferred_element_type=jnp.float32,
        )
        moment[member] = product[:half, :samples] + (
            product[half : 2 * half, :samples] + product[2 * half :, :samples]
        )
        first = product[:half, samples:]
        second = product[half : 2 * half, samples:]
        third = product[2 * half :, samples:]
        turned = jnp.concatenate([third, jnp.zeros_like(third)], axis=0).T[:half]
        small = second + third + turned
        shifted = pltpu.roll(first + second, half, 1)
        start[member] = jnp.where(
            lanes < half, first + (shifted + small), diagonal.astype(jnp.float32)
        )


def gram_call(index, counts, part, source, halo, blocks):
    count, rows, samples = part.shape
    slots = blocks.shape[1]
    half = samples // 2
    together = 4 if count % 4 == 0 else 1
    anywhere = pl.BlockSpec(memory_space=pl.ANY)
    smem = pl.BlockSpec(memory_space=pltpu.SMEM)

    def per_step(*tail):
        return pl.BlockSpec((together, *tail), lambda b: (b, *(0 for _ in tail)))

    return pl.pallas_call(
        gram_kernel,
        grid=(count // together,),
        in_specs=[
            smem,
            smem,
            per_step(rows, samples),
            per_step(rows, samples),
            pl.BlockSpec((count, rows, samples), lambda b: (0, 0, 0)),
            anywhere,
        ],
        out_specs=[per_step(half, samples), per_step(half, samples), per_step(rows, samples)],
        out_shape=[
            jax.ShapeDtypeStruct((count, half, samples), jnp.float32),
            jax.ShapeDtypeStruct((count, half, samples), jnp.float32),
            jax.ShapeDtypeStruct((count, rows, samples), jnp.bfloat16),
        ],
        scratch_shapes=[
            pltpu.VMEM((count, slots, rows, rows), jnp.bfloat16),
            pltpu.VMEM((together, rows, samples), jnp.float32),
            pltpu.SemaphoreType.DMA((count,)),
        ],
        name="gram",
    )(index, counts, part, source, halo, blocks)


def factor(work, first, nodes, low, high, width):
    half, samples = work.shape[1:]
    octets = half // 8
    row8 = lax.broadcasted_iota(jnp.int32, (nodes, 8, samples), 1)

    def spread_row(value, row):
        return jnp.broadcast_to(value[:, row : row + 1, :], value.shape)

    def spread_column(value, lane):
        return jnp.broadcast_to(value[:, :, lane : lane + 1], value.shape)

    def octet(place):
        return work[first : first + nodes, 8 * place : 8 * place + 8, :]

    def put(place, value):
        work[first : first + nodes, 8 * place : 8 * place + 8, :] = value

    for place in range(low, high):
        base = 8 * place
        head = octet(place)
        upper, pivots = head, None
        for begin in range(0, 8, width):
            rows = range(begin, begin + width)
            columns = {row: spread_column(head, base + row) for row in rows}
            for row in rows:
                pivot = spread_row(columns[row], row)
                pivots = pivot if pivots is None else jnp.where(row8 == row, pivot, pivots)
                scaled = jnp.where(row8 == row, 0.0, columns[row] * (1.0 / pivot))
                line = spread_row(head, row)
                if row:
                    upper = jnp.where(row8 == row, line, upper)
                head = head - scaled * line
                for later in range(row + 1, begin + width):
                    columns[later] = columns[later] - scaled * spread_row(columns[later], row)
        put(place, upper * lax.rsqrt(pivots))
        if place + 1 == octets:
            break
        head = head * (1.0 / pivots)
        lines = [spread_row(head, row) for row in range(8)]
        for other in range(place + 1, octets):
            value = octet(other)
            columns = [spread_column(value, base + row) for row in range(8)]
            for row in range(8):
                value = value - columns[row] * lines[row]
            put(other, value)


def packed(gram, moment):
    rows = gram.shape[0] // 2
    half = gram.shape[1] // 2
    lanes = lax.broadcasted_iota(jnp.int32, (rows, 2 * half), 1)
    top = jnp.where(lanes < half, gram[:rows], pltpu.roll(gram[rows:], half, 1))
    return jnp.concatenate([top, moment], axis=0)


def unpacked(value, half):
    rows = half // 2
    lanes = lax.broadcasted_iota(jnp.int32, (half, 2 * half), 1)
    diagonal = lanes - half == lax.broadcasted_iota(jnp.int32, (half, 2 * half), 0)
    gram = jnp.concatenate([value[:rows], pltpu.roll(value[:rows], half, 1)], axis=0)
    return jnp.where(lanes < half, gram, diagonal.astype(jnp.float32))


def tree_kernel(spread, start, moment, work, local, sums, arrived, sent, landed):
    count, half, samples = start.shape
    depth = count.bit_length() - 1
    me = lax.axis_index(AXIS)
    bits = [lax.rem(lax.div(me, 1 << step), 2) for step in range(spread)]
    partners = [me + (1 - 2 * bit) * (1 << step) for step, bit in enumerate(bits)]
    barrier = pltpu.get_barrier_semaphore()
    for partner in partners:
        pl.semaphore_signal(barrier, inc=1, device_id=(partner,), device_id_type=MESH)

    def exchange(step):
        return pltpu.make_async_remote_copy(
            src_ref=sums.at[step],
            dst_ref=arrived.at[step],
            send_sem=sent.at[step],
            recv_sem=landed.at[step],
            device_id=(partners[step],),
            device_id_type=MESH,
        )

    grams = {(0, leaf): start[leaf] for leaf in range(count)}
    moments = {(0, leaf): moment[leaf] for leaf in range(count)}
    for height in range(1, depth + 1):
        for node in range(count >> height):
            for table in (grams, moments):
                table[height, node] = (
                    table[height - 1, 2 * node] + table[height - 1, 2 * node + 1]
                )
    sums[0] = packed(grams[depth, 0], moments[depth, 0])
    pl.semaphore_wait(barrier, spread)
    copies = [exchange(step) for step in range(spread)]
    copies[0].start()

    lanes = lax.broadcasted_iota(jnp.int32, (half, samples), 1)
    diagonal = lanes - half == lax.broadcasted_iota(jnp.int32, (half, samples), 0)
    for leaf in range(count):
        work[leaf] = start[leaf]
    place = count
    for height in range(1, depth + 1):
        local[height - 1] = moments[height, 0]
        for side in range(1 if height == depth else 2):
            work[place] = jnp.where(
                lanes < half, grams[height, side], diagonal.astype(jnp.float32)
            )
            place += 1
    octets = half // 8
    for step in range(spread):
        factor(
            work, 0, place, octets * step // spread, octets * (step + 1) // spread, 4
        )
        copies[step].wait()
        sums[step + 1] = sums[step] + arrived[step]
        if step + 1 < spread:
            copies[step + 1].start()


def tree_call(start, moment, spread):
    count, half, samples = start.shape
    depth = count.bit_length() - 1
    nodes = count + 2 * depth - 1
    rows = half // 2 + half
    vmem = pl.BlockSpec(memory_space=pltpu.VMEM)
    return pl.pallas_call(
        functools.partial(tree_kernel, spread),
        in_specs=[vmem] * 2,
        out_specs=[vmem] * 4,
        out_shape=[
            jax.ShapeDtypeStruct((nodes, half, samples), jnp.float32),
            jax.ShapeDtypeStruct((depth, half, samples), jnp.float32),
            jax.ShapeDtypeStruct((spread + 1, rows, samples), jnp.float32),
            jax.ShapeDtypeStruct((spread, rows, samples), jnp.float32),
        ],
        scratch_shapes=[
            pltpu.SemaphoreType.DMA((spread,)),
            pltpu.SemaphoreType.DMA((spread,)),
        ],
        compiler_params=pltpu.CompilerParams(collective_id=1, has_side_effects=True),
        name="tree",
    )(start, moment)


def out_kernel(work, moment, local, sums, arrived, compact, leaf_out, level_out, tops):
    count, half, samples = moment.shape
    depth = count.bit_length() - 1
    spread = arrived.shape[0]
    me = lax.axis_index(AXIS)
    lanes = lax.broadcasted_iota(jnp.int32, (half, samples), 1)
    triangle = lanes >= lax.broadcasted_iota(jnp.int32, (half, samples), 0)
    corner = triangle & (lanes < half)
    blank = jnp.zeros((half, samples), jnp.float32)

    def solved(matrix, right):
        middle = fine_dot(matrix, jnp.concatenate([blank, right], axis=0))
        return fine_dot(matrix, middle, ((0,), (0,)))[half:]

    def sketch(one, two, answer):
        stacked = jnp.concatenate(
            [jnp.where(corner, one, 0.0), jnp.where(corner, two, 0.0)], axis=0
        )
        return fine_dot(stacked, jnp.concatenate([answer, blank], axis=0))

    for step in range(spread):
        tops[2 * step] = unpacked(arrived[step], half)
        tops[2 * step + 1] = unpacked(sums[step + 1], half)
    factor(tops, 0, 2 * spread, 0, half // 8, 8)

    for leaf in range(count):
        answer = solved(work[leaf], moment[leaf])
        high = answer.astype(jnp.bfloat16)
        low = (answer - high.astype(jnp.float32)).astype(jnp.bfloat16)
        pair = jnp.concatenate([high, low], axis=1)
        both = jnp.dot(
            compact[leaf],
            jnp.concatenate([pair, pair], axis=0),
            preferred_element_type=jnp.float32,
        )
        leaf_out[leaf] = (both[:, :samples] + both[:, samples:]).astype(leaf_out.dtype)
    for height in range(1, depth + 1):
        first = 0 if height == 1 else count + 2 * (height - 2)
        answer = solved(work[count + 2 * (height - 1)], local[height - 1])
        level_out[0, height - 1] = sketch(work[first], work[first + 1], answer).astype(
            level_out.dtype
        )
    for step in range(spread):
        mine = work[count + 2 * (depth - 1)] if step == 0 else tops[2 * step - 1]
        other = tops[2 * step]
        odd = lax.rem(lax.div(me, 1 << step), 2) == 1
        answer = solved(tops[2 * step + 1], sums[step + 1, half // 2 :, :])
        level_out[0, depth + step] = sketch(
            jnp.where(odd, other, mine), jnp.where(odd, mine, other), answer
        ).astype(level_out.dtype)


def out_call(work, moment, local, sums, arrived, compact):
    count, rows, samples = compact.shape
    half = moment.shape[1]
    spread = arrived.shape[0]
    depth = count.bit_length() - 1
    vmem = pl.BlockSpec(memory_space=pltpu.VMEM)
    return pl.pallas_call(
        out_kernel,
        in_specs=[vmem] * 6,
        out_specs=[vmem] * 2,
        out_shape=[
            jax.ShapeDtypeStruct((count, rows, samples), jnp.bfloat16),
            jax.ShapeDtypeStruct((1, depth + spread, samples, samples), jnp.bfloat16),
        ],
        scratch_shapes=[pltpu.VMEM((2 * spread, half, samples), jnp.float32)],
        name="out",
    )(work, moment, local, sums, arrived, compact)


def per_device(random_block, sample_block, near_blocks, near_index, near_count):
    spread = lax.axis_size(AXIS).bit_length() - 1
    part, halo = halo_call(near_index, near_count, random_block, near_blocks, sample_block)
    start, moment, compact = gram_call(
        near_index, near_count, part, random_block, halo, near_blocks
    )
    work, local, sums, arrived = tree_call(start, moment, spread)
    return tuple(out_call(work, moment, local, sums, arrived, compact))


def solution(mesh):
    return jax.shard_map(
        per_device,
        mesh=mesh,
        in_specs=(
            P(AXIS, None, None),
            P(AXIS, None, None),
            P(AXIS, None, None, None),
            P(AXIS, None),
            P(AXIS),
        ),
        out_specs=(P(AXIS, None, None), P(AXIS, None, None, None)),
        check_vma=False,
    )
```

time: 95.4 us -> 77.2 us (0.81)
  Pallas kernels: 80.2 us -> 74.7 us
  local copies, waits for them, and re-layouts: 5.65 us -> 1.36 us
  waiting for transfers between devices: 4.12 us -> 0 us
  starting transfers between devices: 3.76 us -> 0 us
    pallas_call x2 -> x4, Pallas kernels: 80.2 us -> 74.7 us  [the longest x1 35.2 us: tree_call(): pl.pallas_call(functools.partial(tree_kernel, spread), in_specs=[vmem] *...]
    ppermute x2 -> x0, waiting for transfers between devices: 4.12 us -> none  [the longest x1 4.11 us: per_device(): high = lax.ppermute(random_block, 'boxes', backward)]
    ppermute x2 -> x0, starting transfers between devices: 3.76 us -> none  [the longest x1 2.47 us: per_device(): low = lax.ppermute(random_block, 'boxes', forward)]
    unnamed x6 -> x1, local copies, waits for them, and re-layouts: 4.97 us -> 1.36 us
  transfers between devices with their start and end apart: 2 -> 0, of which waited for: 1 -> 0; matrix products, arithmetic and copies ran while one was open for 1% -> 0% of each run, Pallas kernels for 0% -> 0%
where the time goes in v1:
time: 77.2 us; the launch traced here: 76.7 us
  Pallas kernels  74.7 us (97%)
  local copies, waits for them, and re-layouts  1.36 us (2%)
    pallas_call x1, Pallas kernels, tree_call(): pl.pallas_call(functools.partial(tree_kernel, spread), in_specs=[vmem] *...  35.2 us
    pallas_call x1, Pallas kernels, halo_call(): pl.pallas_call(halo_kernel, grid_spec=pltpu.PrefetchScalarGridSpec(num_sc...  21.3 us
    pallas_call x1, Pallas kernels, out_call(): pl.pallas_call(out_kernel, in_specs=[vmem] * 6, out_specs=[vmem] * 2, out...  10.2 us
    pallas_call x1, Pallas kernels, gram_call(): pl.pallas_call(gram_kernel, grid=(count // together,), in_specs=[smem, sm...  8.03 us

profile of v1, /device:TPU:0, one launch (start us, length us, event | category | flops | bytes accessed | tf_op | source)
XLA Modules:
  0.0 76.7 jit_solution(8393511840716162070)
XLA Ops:
  0.6 1.4 %copy.8.index = s32[16,8]{1,0:T(8,128)} copy(s32[16,8]{0,1:T(8,128)} %param.8) | data formatting | bytes 1024 | tf_op args[3]
  2.0 21.3 %halo.1 = (f32[16,256,128]{2,1,0:T(8,128)}, bf16[16,256,128]{2,1,0:T(8,128)(2,1)}) custom-call(s32[16,8]{1,0:T(8,128)} %copy.8.index, s32[16]{0:T(128)} %counts.3, bf16[16,256,128]{2,1,0:T(8,128)(2,1)} %source.3, bf16[16,8,256,256]{3,2,1,0:T(8,128)(2,1)} %blocks.3, bf16[16,256,128]{2,1,0:T(8,128)(2,1)} %sample.1), custom_call_target="tpu_custom_call" | custom-call | tf_op jit(solution)/shard_map/halo/pallas_call | solution.py:94
  23.3 8.0 %gram.1 = (f32[16,64,128]{2,1,0:T(8,128)}, f32[16,64,128]{2,1,0:T(8,128)}, bf16[16,256,128]{2,1,0:T(8,128)(2,1)}) custom-call(s32[16,8]{1,0:T(8,128)} %copy.8.index, s32[16]{0:T(128)} %counts.3, f32[16,256,128]{2,1,0:T(8,128)} %get-tuple-element.11.part, bf16[16,256,128]{2,1,0:T(8,128)(2,1)} %source.3, bf16[16,256,128]{2,1,0:T(8,128)(2,1)} %get-tuple-element.12.halo, ...), custom_call_target="tpu_custom_call" | custom-call | tf_op jit(solution)/shard_map/gram/pallas_call | solution.py:229
  31.3 35.2 %tree.1 = (f32[23,64,128]{2,1,0:T(8,128)}, f32[4,64,128]{2,1,0:T(8,128)}, f32[6,96,128]{2,1,0:T(8,128)}, f32[5,96,128]{2,1,0:T(8,128)}) custom-call(f32[16,64,128]{2,1,0:T(8,128)} %get-tuple-element.13.start, f32[16,64,128]{2,1,0:T(8,128)} %get-tuple-element.14.moment), custom_call_target="tpu_custom_call" | custom-call | tf_op jit(solution)/shard_map/tree/pallas_call | solution.py:380
  66.5 10.2 %out.1 = (bf16[16,256,128]{2,1,0:T(8,128)(2,1)}, bf16[1,9,128,128]{3,2,1,0:T(8,128)(2,1)}) custom-call(f32[23,64,128]{2,1,0:T(8,128)} %get-tuple-element.15.work, f32[16,64,128]{2,1,0:T(8,128)} %get-tuple-element.14.moment, f32[4,64,128]{2,1,0:T(8,128)} %get-tuple-element.16.local, f32[6,96,128]{2,1,0:T(8,128)} %get-tuple-element.17.sums, ...), custom_call_target="tpu_custom_call" | custom-call | tf_op jit(solution)/shard_map/out/pallas_call | solution.py:457

commit v2 on v1

--- a/solution.py
+++ b/solution.py
@@ -17,237 +17,208 @@
     )
 
 
-def halo_kernel(index, counts, source, blocks, sample, part, halo, wide, copy_sem, sent, landed):
-    box = pl.program_id(0)
-    count = source.shape[0]
-    slots, samples = blocks.shape[1], sample.shape[2]
+def halo_kernel(
+    index, counts, source, blocks, sample, part, halo, held, wide, base, loads, arrivals, sent, landed
+):
+    count, slots, rows = held.shape[:3]
+    samples = part.shape[2]
     size = lax.axis_size(AXIS)
     me = lax.axis_index(AXIS)
     core = lax.rem(me, 2)
     partner = me + 1 - 2 * core
     across = me - 1 + 2 * core
     inside = (across >= 0) & (across < size)
-
-    def local_copy():
-        return pltpu.make_async_copy(source, wide.at[pl.ds(0, count)], copy_sem)
-
-    def near_copy():
-        return pltpu.make_async_remote_copy(
-            src_ref=source,
-            dst_ref=wide.at[pl.ds(count, count)],
-            send_sem=sent.at[0],
-            recv_sem=landed.at[0],
-            device_id=(partner,),
-            device_id_type=MESH,
-        )
-
-    def far_copy():
-        return pltpu.make_async_remote_copy(
-            src_ref=source,
-            dst_ref=halo,
-            send_sem=sent.at[1],
-            recv_sem=landed.at[1],
-            device_id=(across,),
-            device_id_type=MESH,
-        )
-
-    @pl.when(box == 0)
+    near_copy = pltpu.make_async_remote_copy(
+        src_ref=source,
+        dst_ref=wide.at[pl.ds(count, count)],
+        send_sem=sent.at[0],
+        recv_sem=landed.at[0],
+        device_id=(partner,),
+        device_id_type=MESH,
+    )
+    far_copy = pltpu.make_async_remote_copy(
+        src_ref=source,
+        dst_ref=halo,
+        send_sem=sent.at[1],
+        recv_sem=landed.at[1],
+        device_id=(across,),
+        device_id_type=MESH,
+    )
+    own_copy = pltpu.make_async_copy(source, wide.at[pl.ds(0, count)], loads.at[0])
+    sample_copy = pltpu.make_async_copy(sample, base, loads.at[1])
+
+    def fetch(box):
+        return pltpu.make_async_copy(blocks.at[box], held.at[box], arrivals.at[box])
+
+    barrier = pltpu.get_barrier_semaphore()
+    pl.semaphore_signal(barrier, inc=1, device_id=(partner,), device_id_type=MESH)
+
+    @pl.when(inside)
     def _():
-        local_copy().start()
-        barrier = pltpu.get_barrier_semaphore()
-        pl.semaphore_signal(barrier, inc=1, device_id=(partner,), device_id_type=MESH)
-
-        @pl.when(inside)
-        def _():
-            pl.semaphore_signal(barrier, inc=1, device_id=(across,), device_id_type=MESH)
-            pl.semaphore_wait(barrier, 2)
-            far_copy().start()
-
-        @pl.when(jnp.logical_not(inside))
-        def _():
-            pl.semaphore_wait(barrier, 1)
-
-        near_copy().start()
-        local_copy().wait()
-        near_copy().wait()
-
-    total = jnp.zeros(sample.shape[1:], jnp.float32)
-    for slot in range(slots):
-        place = index[box, slot] - me * count
-        other = place - (1 - 2 * core) * count
-        own = (place >= 0) & (place < count)
-        beside = (other >= 0) & (other < count)
-        pick = jnp.where(own, place, jnp.where(beside, other + count, 0))
-        keep = ((own | beside) & (slot < counts[box])).astype(jnp.float32).astype(jnp.bfloat16)
-        total += jnp.dot(blocks[0, slot], wide[pick] * keep, preferred_element_type=jnp.float32)
-    part[0] = sample[0].astype(jnp.float32) - total
-
-    @pl.when((box == pl.num_programs(0) - 1) & inside)
+        pl.semaphore_signal(barrier, inc=1, device_id=(across,), device_id_type=MESH)
+        pl.semaphore_wait(barrier, 2)
+        far_copy.start()
+
+    @pl.when(jnp.logical_not(inside))
     def _():
-        far_copy().wait()
+        pl.semaphore_wait(barrier, 1)
+
+    near_copy.start()
+    own_copy.start()
+    sample_copy.start()
+    for box in range(count):
+        fetch(box).start()
+    own_copy.wait()
+    sample_copy.wait()
+    near_copy.wait()
+
+    def near(box, carry):
+        fetch(box).wait()
+        picked = []
+        for slot in range(slots):
+            place = index[slot, box] - me * count
+            other = place - (1 - 2 * core) * count
+            own = (place >= 0) & (place < count)
+            beside = (other >= 0) & (other < count)
+            pick = jnp.where(own, place, jnp.where(beside, other + count, 0))
+            keep = ((own | beside) & (slot < counts[box])).astype(jnp.float32)
+            picked.append(wide[pick] * keep.astype(jnp.bfloat16))
+        part[box] = base[box].astype(jnp.float32) - jnp.dot(
+            jnp.concatenate([held[box, slot] for slot in range(slots)], axis=1),
+            jnp.concatenate(picked, axis=0),
+            preferred_element_type=jnp.float32,
+        )
+        return carry
+
+    lax.fori_loop(0, count, near, 0)
+
+    @pl.when(inside)
+    def _():
+        far_copy.wait()
 
 
 def halo_call(index, counts, source, blocks, sample):
     count, rows, samples = sample.shape
-    slots = blocks.shape[1]
     anywhere = pl.BlockSpec(memory_space=pl.ANY)
+    smem = pl.BlockSpec(memory_space=pltpu.SMEM)
+    vmem = pl.BlockSpec(memory_space=pltpu.VMEM)
     return pl.pallas_call(
         halo_kernel,
-        grid_spec=pltpu.PrefetchScalarGridSpec(
-            num_scalar_prefetch=0,
-            grid=(count,),
-            in_specs=[
-                pl.BlockSpec(memory_space=pltpu.SMEM),
-                pl.BlockSpec(memory_space=pltpu.SMEM),
-                anywhere,
-                pl.BlockSpec((1, slots, rows, rows), lambda b: (b, 0, 0, 0)),
-                pl.BlockSpec((1, rows, samples), lambda b: (b, 0, 0)),
-            ],
-            out_specs=[pl.BlockSpec((1, rows, samples), lambda b: (b, 0, 0)), anywhere],
-            scratch_shapes=[
-                pltpu.VMEM((2 * count, rows, samples), jnp.bfloat16),
-                pltpu.SemaphoreType.DMA,
-                pltpu.SemaphoreType.DMA((2,)),
-                pltpu.SemaphoreType.DMA((2,)),
-            ],
-        ),
+        in_specs=[smem, smem, anywhere, anywhere, anywhere],
+        out_specs=[vmem, anywhere, vmem],
         out_shape=[
             jax.ShapeDtypeStruct(sample.shape, jnp.float32),
             jax.ShapeDtypeStruct(sample.shape, jnp.bfloat16),
-        ],
-        compiler_params=pltpu.CompilerParams(collective_id=0, has_side_effects=True),
+            jax.ShapeDtypeStruct(blocks.shape, jnp.bfloat16),
+        ],
+        scratch_shapes=[
+            pltpu.VMEM((2 * count, rows, samples), jnp.bfloat16),
+            pltpu.VMEM((count, rows, samples), jnp.bfloat16),
+            pltpu.SemaphoreType.DMA((2,)),
+            pltpu.SemaphoreType.DMA((count,)),
+            pltpu.SemaphoreType.DMA((2,)),
+            pltpu.SemaphoreType.DMA((2,)),
+        ],
+        compiler_params=pltpu.CompilerParams(
+            collective_id=0, has_side_effects=True, vmem_limit_bytes=30 * 2**20
+        ),
         name="halo",
     )(index, counts, source, blocks, sample)
 
 
-def split_three(value):
-    high = value.astype(jnp.bfloat16)
-    rest = value - high.astype(jnp.float32)
-    middle = rest.astype(jnp.bfloat16)
-    low = (rest - middle.astype(jnp.float32)).astype(jnp.bfloat16)
-    return high, middle, low
-
-
-def gram_kernel(index, counts, part, source, halo, blocks, start, moment, compact, held, far, sems):
-    step = pl.program_id(0)
-    steps = pl.num_programs(0)
-    together, rows, samples = part.shape
-    count = halo.shape[0]
-    slots = held.shape[1]
+def gram_kernel(
+    index, counts, part, source, halo, blocks, start, moment, compact, far, picks
+):
+    count, rows, samples = far.shape
+    slots = blocks.shape[1]
     half = samples // 2
     me = lax.axis_index(AXIS)
     core = lax.rem(me, 2)
     base = (me - 1 + 2 * core) * count
 
-    def wanted(box, slot):
-        place = index[box, slot] - base
-        return place, (place >= 0) & (place < count) & (slot < counts[box])
-
-    def fetch(box, slot):
-        return pltpu.make_async_copy(blocks.at[box, slot], held.at[box, slot], sems.at[box])
-
-    def issue(which):
-        for member in range(together):
-            box = which * together + member
-            for slot in range(1, slots):
-                place, needed = wanted(box, slot)
-
-                @pl.when(needed)
-                def _():
-                    fetch(box, slot).start()
-
-    @pl.when(step == 0)
-    def _():
-        issue(0)
-
-    @pl.when(step + 1 < steps)
-    def _():
-        issue(step + 1)
-
-    for member in range(together):
-        box = step * together + member
-        far[member] = part[member]
+    found = jnp.int32(0)
+    for box in range(count):
+        far[box] = part[box]
         for slot in range(1, slots):
-            place, needed = wanted(box, slot)
-
-            @pl.when(needed)
-            def _():
-                fetch(box, slot).wait()
-
-        for slot in range(1, slots):
-            place, needed = wanted(box, slot)
-
-            @pl.when(needed)
-            def _():
-                far[member] -= jnp.dot(
-                    held[box, slot], halo[place], preferred_element_type=jnp.float32
+            place = index[slot, box] - base
+            needed = (place >= 0) & (place < count) & (slot < counts[box])
+            picks[found] = (box * slots + slot) * count + place
+            found = found + needed.astype(jnp.int32)
+    group = 4
+
+    def multiply(turn, carry):
+        terms = []
+        for member in range(group):
+            entry = turn * group + member
+            code = picks[jnp.minimum(entry, found - 1)]
+            block = lax.div(code, count)
+            box = lax.div(block, slots)
+            keep = (entry < found).astype(jnp.float32).astype(jnp.bfloat16)
+            terms.append(
+                (
+                    box,
+                    jnp.dot(
+                        blocks[box, lax.rem(block, slots)],
+                        halo[lax.rem(code, count)] * keep,
+                        preferred_element_type=jnp.float32,
+                    ),
                 )
+            )
+        for box, term in terms:
+            far[box] -= term
+        return carry
+
+    lax.fori_loop(0, lax.div(found + group - 1, group), multiply, 0)
 
     lanes_rows = lax.broadcasted_iota(jnp.int32, (rows, samples), 1)
     lanes = lax.broadcasted_iota(jnp.int32, (half, samples), 1)
     diagonal = lanes - half == lax.broadcasted_iota(jnp.int32, (half, samples), 0)
-    for member in range(together):
-        value = far[member]
-        doubled = value + pltpu.roll(value, half, 1)
-        flipped = doubled.T[:half]
-        high, middle, low = split_three(flipped)
-        left = jnp.concatenate([high, middle, low], axis=0)
-        top = doubled.astype(jnp.bfloat16)
-        next_top = doubled - top.astype(jnp.float32)
-        both = jnp.where(lanes_rows < half, top.astype(jnp.float32), next_top).astype(jnp.bfloat16)
-        compact[member] = both
-        product = jnp.dot(
-            left,
-            jnp.concatenate([source[member], both], axis=1),
-            preferred_element_type=jnp.float32,
-        )
-        moment[member] = product[:half, :samples] + (
-            product[half : 2 * half, :samples] + product[2 * half :, :samples]
-        )
-        first = product[:half, samples:]
-        second = product[half : 2 * half, samples:]
-        third = product[2 * half :, samples:]
-        turned = jnp.concatenate([third, jnp.zeros_like(third)], axis=0).T[:half]
-        small = second + third + turned
-        shifted = pltpu.roll(first + second, half, 1)
-        start[member] = jnp.where(
-            lanes < half, first + (shifted + small), diagonal.astype(jnp.float32)
-        )
+    together = 4 if count % 4 == 0 else 1
+
+    def reduce(turn, carry):
+        for member in range(together):
+            box = turn * together + member
+            value = far[box]
+            doubled = value + pltpu.roll(value, half, 1)
+            high = doubled.astype(jnp.bfloat16).astype(jnp.float32)
+            both = jnp.where(lanes_rows < half, high, doubled - high).astype(jnp.bfloat16)
+            compact[box] = both
+            product = jnp.dot(
+                both.T,
+                jnp.concatenate([source[box], both], axis=1),
+                preferred_element_type=jnp.float32,
+            )
+            moment[box] = product[:half, :samples] + product[half:, :samples]
+            mixed = product[:half, samples:] + product[half:, samples:]
+            start[box] = jnp.where(
+                lanes < half, mixed + pltpu.roll(mixed, half, 1), diagonal.astype(jnp.float32)
+            )
+        return carry
+
+    lax.fori_loop(0, count // together, reduce, 0)
 
 
 def gram_call(index, counts, part, source, halo, blocks):
     count, rows, samples = part.shape
     slots = blocks.shape[1]
     half = samples // 2
-    together = 4 if count % 4 == 0 else 1
-    anywhere = pl.BlockSpec(memory_space=pl.ANY)
+    most = count * (slots - 1)
     smem = pl.BlockSpec(memory_space=pltpu.SMEM)
-
-    def per_step(*tail):
-        return pl.BlockSpec((together, *tail), lambda b: (b, *(0 for _ in tail)))
-
+    vmem = pl.BlockSpec(memory_space=pltpu.VMEM)
     return pl.pallas_call(
         gram_kernel,
-        grid=(count // together,),
-        in_specs=[
-            smem,
-            smem,
-            per_step(rows, samples),
-            per_step(rows, samples),
-            pl.BlockSpec((count, rows, samples), lambda b: (0, 0, 0)),
-            anywhere,
-        ],
-        out_specs=[per_step(half, samples), per_step(half, samples), per_step(rows, samples)],
+        in_specs=[smem, smem, vmem, vmem, vmem, vmem],
+        out_specs=[vmem] * 3,
         out_shape=[
             jax.ShapeDtypeStruct((count, half, samples), jnp.float32),
             jax.ShapeDtypeStruct((count, half, samples), jnp.float32),
             jax.ShapeDtypeStruct((count, rows, samples), jnp.bfloat16),
         ],
         scratch_shapes=[
-            pltpu.VMEM((count, slots, rows, rows), jnp.bfloat16),
-            pltpu.VMEM((together, rows, samples), jnp.float32),
-            pltpu.SemaphoreType.DMA((count,)),
-        ],
+            pltpu.VMEM((count, rows, samples), jnp.float32),
+            pltpu.SMEM((most + 1,), jnp.int32),
+        ],
+        compiler_params=pltpu.CompilerParams(vmem_limit_bytes=12 * 2**20),
         name="gram",
     )(index, counts, part, source, halo, blocks)
 
@@ -261,7 +232,8 @@
         return jnp.broadcast_to(value[:, row : row + 1, :], value.shape)
 
     def spread_column(value, lane):
-        return jnp.broadcast_to(value[:, :, lane : lane + 1], value.shape)
+        flat = value.reshape(nodes * 8, samples)
+        return jnp.broadcast_to(flat[:, lane : lane + 1], flat.shape).reshape(value.shape)
 
     def octet(place):
         return work[first : first + nodes, 8 * place : 8 * place + 8, :]
@@ -391,7 +363,9 @@
             pltpu.SemaphoreType.DMA((spread,)),
             pltpu.SemaphoreType.DMA((spread,)),
         ],
-        compiler_params=pltpu.CompilerParams(collective_id=1, has_side_effects=True),
+        compiler_params=pltpu.CompilerParams(
+            collective_id=1, has_side_effects=True, vmem_limit_bytes=12 * 2**20
+        ),
         name="tree",
     )(start, moment)
 
@@ -463,15 +437,17 @@
             jax.ShapeDtypeStruct((1, depth + spread, samples, samples), jnp.bfloat16),
         ],
         scratch_shapes=[pltpu.VMEM((2 * spread, half, samples), jnp.float32)],
+        compiler_params=pltpu.CompilerParams(vmem_limit_bytes=12 * 2**20),
         name="out",
     )(work, moment, local, sums, arrived, compact)
 
 
 def per_device(random_block, sample_block, near_blocks, near_index, near_count):
     spread = lax.axis_size(AXIS).bit_length() - 1
-    part, halo = halo_call(near_index, near_count, random_block, near_blocks, sample_block)
+    index = near_index.T
+    part, halo, held = halo_call(index, near_count, random_block, near_blocks, sample_block)
     start, moment, compact = gram_call(
-        near_index, near_count, part, random_block, halo, near_blocks
+        index, near_count, part, random_block, halo, held
     )
     work, local, sums, arrived = tree_call(start, moment, spread)
     return tuple(out_call(work, moment, local, sums, arrived, compact))

time: 77.2 us -> 64.7 us (0.84)
  Pallas kernels: 74.7 us -> 60.4 us
  local copies, waits for them, and re-layouts: 1.36 us -> 3.78 us
    pallas_call x2, Pallas kernels: 29.3 us -> 16.3 us  [the longest x1 13.3 us: halo_call(): pl.pallas_call(halo_kernel, in_specs=[smem, smem, anywhere, anywhere, any...]
    unnamed x1 -> x8, local copies, waits for them, and re-layouts: 1.36 us -> 3.78 us
    pallas_call x1, Pallas kernels: 10.2 us -> 8.18 us  [out_call(): pl.pallas_call(out_kernel, in_specs=[vmem] * 6, out_specs=[vmem] * 2, out...]
where the time goes in v2:
time: 64.7 us; the launch traced here: 64.8 us
  Pallas kernels  60.4 us (93%)
  local copies, waits for them, and re-layouts  3.78 us (6%)
  between operations  0.67 us (1%)
    pallas_call x1, Pallas kernels, tree_call(): pl.pallas_call(functools.partial(tree_kernel, spread), in_specs=[vmem] *...  35.9 us
    pallas_call x1, Pallas kernels, halo_call(): pl.pallas_call(halo_kernel, in_specs=[smem, smem, anywhere, anywhere, any...  13.3 us
    pallas_call x1, Pallas kernels, out_call(): pl.pallas_call(out_kernel, in_specs=[vmem] * 6, out_specs=[vmem] * 2, out...  8.18 us
    unnamed x8, local copies, waits for them, and re-layouts  3.78 us
    pallas_call x1, Pallas kernels, gram_call(): pl.pallas_call(gram_kernel, in_specs=[smem, smem, vmem, vmem, vmem, vmem]...  3.05 us

profile of v2, /device:TPU:0, one launch (start us, length us, event | category | flops | bytes accessed | tf_op | source)
XLA Modules:
  0.0 64.8 jit_solution(3150085488147636443)
XLA Ops:
  0.6 0.0 copy-start
  0.6 1.2 %copy-done = bf16[16,256,128]{2,1,0:T(8,128)(2,1)S(1)} copy-done((bf16[16,256,128]{2,1,0:T(8,128)(2,1)S(1)}, bf16[16,256,128]{2,1,0:T(8,128)(2,1)}, u32[]{:S(2)}) %copy-start) | copy-done | bytes 1048600
  1.9 0.0 copy-start.1
  1.9 1.2 %copy-done.1 = bf16[16,256,128]{2,1,0:T(8,128)(2,1)S(1)} copy-done((bf16[16,256,128]{2,1,0:T(8,128)(2,1)S(1)}, bf16[16,256,128]{2,1,0:T(8,128)(2,1)}, u32[]{:S(2)}) %copy-start.1) | copy-done | bytes 1048600
  3.1 0.0 copy-start.2
  3.1 0.7 %copy-done.2 = s32[16,8]{0,1:T(8,128)S(1)} copy-done((s32[16,8]{0,1:T(8,128)S(1)}, s32[16,8]{0,1:T(8,128)}, u32[]{:S(2)}) %copy-start.2) | copy-done | bytes 536
  3.8 0.0 copy-start.3
  3.8 0.7 %copy-done.3 = s32[16]{0:T(128)S(1)} copy-done((s32[16]{0:T(128)S(1)}, s32[16]{0:T(128)}, u32[]{:S(2)}) %copy-start.3) | copy-done | bytes 88
  4.4 13.3 %halo.1 = (f32[16,256,128]{2,1,0:T(8,128)S(1)}, bf16[16,256,128]{2,1,0:T(8,128)(2,1)S(1)}, bf16[16,8,256,256]{3,2,1,0:T(8,128)(2,1)S(1)}) custom-call(s32[8,16]{1,0:T(8,128)S(1)} %bitcast.1, s32[16]{0:T(128)S(1)} %copy-done.3, bf16[16,256,128]{2,1,0:T(8,128)(2,1)S(1)} %copy-done, bf16[16,8,256,256]{3,2,1,0:T(8,128)(2,1)} %blocks.1, ...), custom_call_target="tpu_custom_call" | custom-call | tf_op jit(solution)/shard_map/halo/pallas_call | solution.py:105
  17.7 3.0 %gram.1 = (f32[16,64,128]{2,1,0:T(8,128)S(1)}, f32[16,64,128]{2,1,0:T(8,128)S(1)}, bf16[16,256,128]{2,1,0:T(8,128)(2,1)S(1)}) custom-call(s32[8,16]{1,0:T(8,128)S(1)} %bitcast.2, s32[16]{0:T(128)S(1)} %copy-done.3, f32[16,256,128]{2,1,0:T(8,128)S(1)} %get-tuple-element.12.part, bf16[16,256,128]{2,1,0:T(8,128)(2,1)S(1)} %copy-done, ...), custom_call_target="tpu_custom_call" | custom-call | tf_op jit(solution)/shard_map/gram/pallas_call | solution.py:208
  20.7 35.9 %tree.1 = (f32[23,64,128]{2,1,0:T(8,128)S(1)}, f32[4,64,128]{2,1,0:T(8,128)S(1)}, f32[6,96,128]{2,1,0:T(8,128)S(1)}, f32[5,96,128]{2,1,0:T(8,128)S(1)}) custom-call(f32[16,64,128]{2,1,0:T(8,128)S(1)} %get-tuple-element.15.start, f32[16,64,128]{2,1,0:T(8,128)S(1)} %get-tuple-element.16.moment), custom_call_target="tpu_custom_call" | custom-call | tf_op jit(solution)/shard_map/tree/pallas_call | solution.py:352
  56.6 8.2 %out.1 = (bf16[16,256,128]{2,1,0:T(8,128)(2,1)}, bf16[1,9,128,128]{3,2,1,0:T(8,128)(2,1)}) custom-call(f32[23,64,128]{2,1,0:T(8,128)S(1)} %get-tuple-element.17.work, f32[16,64,128]{2,1,0:T(8,128)S(1)} %get-tuple-element.16.moment, f32[4,64,128]{2,1,0:T(8,128)S(1)} %get-tuple-element.18.local, f32[6,96,128]{2,1,0:T(8,128)S(1)} %get-tuple-element.19.sums, ...), custom_call_target="tpu_custom_call" | custom-call | tf_op jit(solution)/shard_map/out/pallas_call | solution.py:431
Async XLA Ops:
  0.6 1.2 %copy-start = (bf16[16,256,128]{2,1,0:T(8,128)(2,1)S(1)}, bf16[16,256,128]{2,1,0:T(8,128)(2,1)}, u32[]{:S(2)}) copy-start(bf16[16,256,128]{2,1,0:T(8,128)(2,1)} %source.3) | copy-start | bytes 3145732
  1.9 1.2 %copy-start.1 = (bf16[16,256,128]{2,1,0:T(8,128)(2,1)S(1)}, bf16[16,256,128]{2,1,0:T(8,128)(2,1)}, u32[]{:S(2)}) copy-start(bf16[16,256,128]{2,1,0:T(8,128)(2,1)} %sample.1) | copy-start | bytes 3145732
  3.1 0.7 %copy-start.2 = (s32[16,8]{0,1:T(8,128)S(1)}, s32[16,8]{0,1:T(8,128)}, u32[]{:S(2)}) copy-start(s32[16,8]{0,1:T(8,128)} %param.8) | copy-start | bytes 1540
  3.8 0.7 %copy-start.3 = (s32[16]{0:T(128)S(1)}, s32[16]{0:T(128)}, u32[]{:S(2)}) copy-start(s32[16]{0:T(128)} %counts.3) | copy-start | bytes 196

commit v3 on v2

--- a/solution.py
+++ b/solution.py
@@ -18,7 +18,22 @@
 
 
 def halo_kernel(
-    index, counts, source, blocks, sample, part, halo, held, wide, base, loads, arrivals, sent, landed
+    lists,
+    lengths,
+    source,
+    blocks,
+    sample,
+    part,
+    halo,
+    held,
+    wide,
+    base,
+    index,
+    counts,
+    loads,
+    arrivals,
+    sent,
+    landed,
 ):
     count, slots, rows = held.shape[:3]
     samples = part.shape[2]
@@ -46,6 +61,9 @@
     )
     own_copy = pltpu.make_async_copy(source, wide.at[pl.ds(0, count)], loads.at[0])
     sample_copy = pltpu.make_async_copy(sample, base, loads.at[1])
+    list_copy = pltpu.make_async_copy(lists, index, loads.at[2])
+    length_copy = pltpu.make_async_copy(lengths, counts, loads.at[3])
+    own_copies = (own_copy, sample_copy, list_copy, length_copy)
 
     def fetch(box):
         return pltpu.make_async_copy(blocks.at[box], held.at[box], arrivals.at[box])
@@ -64,12 +82,12 @@
         pl.semaphore_wait(barrier, 1)
 
     near_copy.start()
-    own_copy.start()
-    sample_copy.start()
+    for copy in own_copies:
+        copy.start()
     for box in range(count):
         fetch(box).start()
-    own_copy.wait()
-    sample_copy.wait()
+    for copy in own_copies:
+        copy.wait()
     near_copy.wait()
 
     def near(box, carry):
@@ -100,11 +118,11 @@
 def halo_call(index, counts, source, blocks, sample):
     count, rows, samples = sample.shape
     anywhere = pl.BlockSpec(memory_space=pl.ANY)
-    smem = pl.BlockSpec(memory_space=pltpu.SMEM)
+    fixed = pl.BlockSpec(memory_space=pltpu.HBM)
     vmem = pl.BlockSpec(memory_space=pltpu.VMEM)
     return pl.pallas_call(
         halo_kernel,
-        in_specs=[smem, smem, anywhere, anywhere, anywhere],
+        in_specs=[fixed] * 5,
         out_specs=[vmem, anywhere, vmem],
         out_shape=[
             jax.ShapeDtypeStruct(sample.shape, jnp.float32),
@@ -114,7 +132,9 @@
         scratch_shapes=[
             pltpu.VMEM((2 * count, rows, samples), jnp.bfloat16),
             pltpu.VMEM((count, rows, samples), jnp.bfloat16),
-            pltpu.SemaphoreType.DMA((2,)),
+            pltpu.SMEM(index.shape, jnp.int32),
+            pltpu.SMEM(counts.shape, jnp.int32),
+            pltpu.SemaphoreType.DMA((4,)),
             pltpu.SemaphoreType.DMA((count,)),
             pltpu.SemaphoreType.DMA((2,)),
             pltpu.SemaphoreType.DMA((2,)),
@@ -393,19 +413,20 @@
     for step in range(spread):
         tops[2 * step] = unpacked(arrived[step], half)
         tops[2 * step + 1] = unpacked(sums[step + 1], half)
-    factor(tops, 0, 2 * spread, 0, half // 8, 8)
-
-    for leaf in range(count):
-        answer = solved(work[leaf], moment[leaf])
-        high = answer.astype(jnp.bfloat16)
-        low = (answer - high.astype(jnp.float32)).astype(jnp.bfloat16)
-        pair = jnp.concatenate([high, low], axis=1)
-        both = jnp.dot(
-            compact[leaf],
-            jnp.concatenate([pair, pair], axis=0),
-            preferred_element_type=jnp.float32,
-        )
-        leaf_out[leaf] = (both[:, :samples] + both[:, samples:]).astype(leaf_out.dtype)
+    octets = half // 8
+    for turn in range(octets):
+        factor(tops, 0, 2 * spread, turn, turn + 1, 8)
+        for leaf in range(count * turn // octets, count * (turn + 1) // octets):
+            answer = solved(work[leaf], moment[leaf])
+            high = answer.astype(jnp.bfloat16)
+            low = (answer - high.astype(jnp.float32)).astype(jnp.bfloat16)
+            pair = jnp.concatenate([high, low], axis=1)
+            both = jnp.dot(
+                compact[leaf],
+                jnp.concatenate([pair, pair], axis=0),
+                preferred_element_type=jnp.float32,
+            )
+            leaf_out[leaf] = (both[:, :samples] + both[:, samples:]).astype(leaf_out.dtype)
     for height in range(1, depth + 1):
         first = 0 if height == 1 else count + 2 * (height - 2)
         answer = solved(work[count + 2 * (height - 1)], local[height - 1])
@@ -445,7 +466,11 @@
 def per_device(random_block, sample_block, near_blocks, near_index, near_count):
     spread = lax.axis_size(AXIS).bit_length() - 1
     index = near_index.T
-    part, halo, held = halo_call(index, near_count, random_block, near_blocks, sample_block)
+    fixed = [
+        pltpu.with_memory_space_constraint(value, pltpu.HBM)
+        for value in (index, near_count, random_block, near_blocks, sample_block)
+    ]
+    part, halo, held = halo_call(*fixed)
     start, moment, compact = gram_call(
         index, near_count, part, random_block, halo, held
     )

time: 64.7 us -> 61.1 us (0.944)
  local copies, waits for them, and re-layouts: 3.78 us -> 0.01 us
    unnamed x8 -> x6, local copies, waits for them, and re-layouts: 3.78 us -> 0.01 us
    pallas_call x1, Pallas kernels: 35.9 us -> 34.5 us  [tree_call(): pl.pallas_call(functools.partial(tree_kernel, spread), in_specs=[vmem] *...]
    pallas_call x1, Pallas kernels: 13.3 us -> 14.1 us  [halo_call(): pl.pallas_call(halo_kernel, in_specs=[fixed] * 5, out_specs=[vmem, anywhe...]
where the time goes in v3:
time: 61.1 us; the launch traced here: 60.6 us
  Pallas kernels  59.9 us (98%)
  between operations  0.7 us (1%)
    pallas_call x1, Pallas kernels, tree_call(): pl.pallas_call(functools.partial(tree_kernel, spread), in_specs=[vmem] *...  34.5 us
    pallas_call x1, Pallas kernels, halo_call(): pl.pallas_call(halo_kernel, in_specs=[fixed] * 5, out_specs=[vmem, anywhe...  14.1 us
    pallas_call x1, Pallas kernels, out_call(): pl.pallas_call(out_kernel, in_specs=[vmem] * 6, out_specs=[vmem] * 2, out...  8.25 us
    pallas_call x1, Pallas kernels, gram_call(): pl.pallas_call(gram_kernel, in_specs=[smem, smem, vmem, vmem, vmem, vmem]...  3.04 us

profile of v3, /device:TPU:0, one launch (start us, length us, event | category | flops | bytes accessed | tf_op | source)
XLA Modules:
  0.0 60.6 jit_solution(10516222177506016519)
XLA Ops:
  0.6 0.0 copy-start.2
  0.6 0.0 copy-start
  0.7 0.0 copy-start.1
  0.7 14.1 %halo.1 = (f32[16,256,128]{2,1,0:T(8,128)S(1)}, bf16[16,256,128]{2,1,0:T(8,128)(2,1)S(1)}, bf16[16,8,256,256]{3,2,1,0:T(8,128)(2,1)S(1)}) custom-call(s32[8,16]{1,0:T(8,128)} %bitcast.1, s32[16]{0:T(128)} %counts.1, bf16[16,256,128]{2,1,0:T(8,128)(2,1)} %source.3, bf16[16,8,256,256]{3,2,1,0:T(8,128)(2,1)} %blocks.1, bf16[16,256,128]{2,1,0:T(8,128)(2,1)} %sample.1), custom_call_target="tpu_custom_call" | custom-call | tf_op jit(solution)/shard_map/halo/pallas_call | solution.py:123
  14.7 0.0 copy-done.2
  14.8 0.0 copy-done
  14.8 0.0 copy-done.1
  14.8 3.0 %gram.1 = (f32[16,64,128]{2,1,0:T(8,128)S(1)}, f32[16,64,128]{2,1,0:T(8,128)S(1)}, bf16[16,256,128]{2,1,0:T(8,128)(2,1)S(1)}) custom-call(s32[8,16]{1,0:T(8,128)S(1)} %bitcast.2, s32[16]{0:T(128)S(1)} %copy-done.2, f32[16,256,128]{2,1,0:T(8,128)S(1)} %get-tuple-element.12.part, bf16[16,256,128]{2,1,0:T(8,128)(2,1)S(1)} %copy-done, ...), custom_call_target="tpu_custom_call" | custom-call | tf_op jit(solution)/shard_map/gram/pallas_call | solution.py:228
  17.8 34.5 %tree.1 = (f32[23,64,128]{2,1,0:T(8,128)S(1)}, f32[4,64,128]{2,1,0:T(8,128)S(1)}, f32[6,96,128]{2,1,0:T(8,128)S(1)}, f32[5,96,128]{2,1,0:T(8,128)S(1)}) custom-call(f32[16,64,128]{2,1,0:T(8,128)S(1)} %get-tuple-element.15.start, f32[16,64,128]{2,1,0:T(8,128)S(1)} %get-tuple-element.16.moment), custom_call_target="tpu_custom_call" | custom-call | tf_op jit(solution)/shard_map/tree/pallas_call | solution.py:372
  52.4 8.3 %out.1 = (bf16[16,256,128]{2,1,0:T(8,128)(2,1)}, bf16[1,9,128,128]{3,2,1,0:T(8,128)(2,1)}) custom-call(f32[23,64,128]{2,1,0:T(8,128)S(1)} %get-tuple-element.17.work, f32[16,64,128]{2,1,0:T(8,128)S(1)} %get-tuple-element.16.moment, f32[4,64,128]{2,1,0:T(8,128)S(1)} %get-tuple-element.18.local, f32[6,96,128]{2,1,0:T(8,128)S(1)} %get-tuple-element.19.sums, ...), custom_call_target="tpu_custom_call" | custom-call | tf_op jit(solution)/shard_map/out/pallas_call | solution.py:452
Async XLA Ops:
  0.6 14.1 %copy-start.2 = (s32[16]{0:T(128)S(1)}, s32[16]{0:T(128)}, u32[]{:S(2)}) copy-start(s32[16]{0:T(128)} %counts.1) | copy-start | bytes 196
  0.6 14.1 %copy-start = (bf16[16,256,128]{2,1,0:T(8,128)(2,1)S(1)}, bf16[16,256,128]{2,1,0:T(8,128)(2,1)}, u32[]{:S(2)}) copy-start(bf16[16,256,128]{2,1,0:T(8,128)(2,1)} %source.3) | copy-start | bytes 3145732
  0.7 14.1 %copy-start.1 = (s32[16,8]{0,1:T(8,128)S(1)}, s32[16,8]{0,1:T(8,128)}, u32[]{:S(2)}) copy-start(s32[16,8]{0,1:T(8,128)} %param.8) | copy-start | bytes 1540

commit v4 on v3

--- a/solution.py
+++ b/solution.py
@@ -243,7 +243,7 @@
     )(index, counts, part, source, halo, blocks)
 
 
-def factor(work, first, nodes, low, high, width):
+def factor(work, nodes, low, high, width):
     half, samples = work.shape[1:]
     octets = half // 8
     row8 = lax.broadcasted_iota(jnp.int32, (nodes, 8, samples), 1)
@@ -255,40 +255,48 @@
         flat = value.reshape(nodes * 8, samples)
         return jnp.broadcast_to(flat[:, lane : lane + 1], flat.shape).reshape(value.shape)
 
-    def octet(place):
-        return work[first : first + nodes, 8 * place : 8 * place + 8, :]
-
-    def put(place, value):
-        work[first : first + nodes, 8 * place : 8 * place + 8, :] = value
-
     for place in range(low, high):
         base = 8 * place
-        head = octet(place)
-        upper, pivots = head, None
+        head = work[:nodes, base : base + 8, :]
+        pivots = None
         for begin in range(0, 8, width):
             rows = range(begin, begin + width)
             columns = {row: spread_column(head, base + row) for row in rows}
             for row in rows:
                 pivot = spread_row(columns[row], row)
-                pivots = pivot if pivots is None else jnp.where(row8 == row, pivot, pivots)
-                scaled = jnp.where(row8 == row, 0.0, columns[row] * (1.0 / pivot))
-                line = spread_row(head, row)
-                if row:
-                    upper = jnp.where(row8 == row, line, upper)
-                head = head - scaled * line
+                pivots = pivot if pivots is None else jnp.where(row8 >= row, pivot, pivots)
+                if row == 7:
+                    break
+                scaled = jnp.where(row8 > row, columns[row] * (1.0 / pivot), 0.0)
+                head = head - scaled * spread_row(head, row)
                 for later in range(row + 1, begin + width):
                     columns[later] = columns[later] - scaled * spread_row(columns[later], row)
-        put(place, upper * lax.rsqrt(pivots))
+        root = head * lax.rsqrt(pivots)
+        work[:nodes, base : base + 8, :] = root
         if place + 1 == octets:
             break
-        head = head * (1.0 / pivots)
-        lines = [spread_row(head, row) for row in range(8)]
-        for other in range(place + 1, octets):
-            value = octet(other)
-            columns = [spread_column(value, base + row) for row in range(8)]
-            for row in range(8):
-                value = value - columns[row] * lines[row]
-            put(other, value)
+        high_part = root.astype(jnp.bfloat16).astype(jnp.float32)
+        rest = root - high_part
+        middle = rest.astype(jnp.bfloat16).astype(jnp.float32)
+        low_part = rest - middle
+        for node in range(nodes):
+            h, m, t = high_part[node], middle[node], low_part[node]
+            left = jnp.concatenate([h, h, m, m, h, t], axis=0).astype(jnp.bfloat16)
+            right = jnp.concatenate([h, m, h, m, t, h], axis=0).astype(jnp.bfloat16)
+            update = lax.dot_general(
+                left[:, :half],
+                right,
+                (((0,), (0,)), ((), ())),
+                preferred_element_type=jnp.float32,
+            )
+            work[node, base + 8 :, :] = work[node, base + 8 :, :] - update[base + 8 :, :]
+
+
+def solved(matrix, right):
+    half = right.shape[0]
+    blank = jnp.zeros_like(right)
+    middle = fine_dot(matrix, jnp.concatenate([blank, right], axis=0))
+    return fine_dot(matrix, middle, ((0,), (0,)))[half:]
 
 
 def packed(gram, moment):
@@ -307,7 +315,7 @@
     return jnp.where(lanes < half, gram, diagonal.astype(jnp.float32))
 
 
-def tree_kernel(spread, start, moment, work, local, sums, arrived, sent, landed):
+def tree_kernel(spread, start, moment, work, answers, sums, arrived, sent, landed):
     count, half, samples = start.shape
     depth = count.bit_length() - 1
     me = lax.axis_index(AXIS)
@@ -345,18 +353,22 @@
     for leaf in range(count):
         work[leaf] = start[leaf]
     place = count
+    targets = [(leaf, moments[0, leaf]) for leaf in range(count)]
     for height in range(1, depth + 1):
-        local[height - 1] = moments[height, 0]
+        targets.append((place, moments[height, 0]))
         for side in range(1 if height == depth else 2):
             work[place] = jnp.where(
                 lanes < half, grams[height, side], diagonal.astype(jnp.float32)
             )
             place += 1
     octets = half // 8
+    turns = max(spread - 1, 1)
     for step in range(spread):
-        factor(
-            work, 0, place, octets * step // spread, octets * (step + 1) // spread, 4
-        )
+        if step < turns:
+            factor(work, place, octets * step // turns, octets * (step + 1) // turns, 4)
+        if step == spread - 1:
+            for row, (node, right) in enumerate(targets):
+                answers[row] = solved(work[node], right)
         copies[step].wait()
         sums[step + 1] = sums[step] + arrived[step]
         if step + 1 < spread:
@@ -375,7 +387,7 @@
         out_specs=[vmem] * 4,
         out_shape=[
             jax.ShapeDtypeStruct((nodes, half, samples), jnp.float32),
-            jax.ShapeDtypeStruct((depth, half, samples), jnp.float32),
+            jax.ShapeDtypeStruct((count + depth, half, samples), jnp.float32),
             jax.ShapeDtypeStruct((spread + 1, rows, samples), jnp.float32),
             jax.ShapeDtypeStruct((spread, rows, samples), jnp.float32),
         ],
@@ -390,8 +402,11 @@
     )(start, moment)
 
 
-def out_kernel(work, moment, local, sums, arrived, compact, leaf_out, level_out, tops):
-    count, half, samples = moment.shape
+def out_kernel(
+    work, answers, sums, arrived, compact, leaf_out, level_out, tops, leaves, sems
+):
+    count, rows, samples = compact.shape
+    half = answers.shape[1]
     depth = count.bit_length() - 1
     spread = arrived.shape[0]
     me = lax.axis_index(AXIS)
@@ -400,10 +415,6 @@
     corner = triangle & (lanes < half)
     blank = jnp.zeros((half, samples), jnp.float32)
 
-    def solved(matrix, right):
-        middle = fine_dot(matrix, jnp.concatenate([blank, right], axis=0))
-        return fine_dot(matrix, middle, ((0,), (0,)))[half:]
-
     def sketch(one, two, answer):
         stacked = jnp.concatenate(
             [jnp.where(corner, one, 0.0), jnp.where(corner, two, 0.0)], axis=0
@@ -414,10 +425,12 @@
         tops[2 * step] = unpacked(arrived[step], half)
         tops[2 * step + 1] = unpacked(sums[step + 1], half)
     octets = half // 8
+    copies = []
     for turn in range(octets):
-        factor(tops, 0, 2 * spread, turn, turn + 1, 8)
-        for leaf in range(count * turn // octets, count * (turn + 1) // octets):
-            answer = solved(work[leaf], moment[leaf])
+        factor(tops, 2 * spread, turn, turn + 1, 8)
+        first, last = count * turn // octets, count * (turn + 1) // octets
+        for leaf in range(first, last):
+            answer = answers[leaf]
             high = answer.astype(jnp.bfloat16)
             low = (answer - high.astype(jnp.float32)).astype(jnp.bfloat16)
             pair = jnp.concatenate([high, low], axis=1)
@@ -426,13 +439,17 @@
                 jnp.concatenate([pair, pair], axis=0),
                 preferred_element_type=jnp.float32,
             )
-            leaf_out[leaf] = (both[:, :samples] + both[:, samples:]).astype(leaf_out.dtype)
+            leaves[leaf] = (both[:, :samples] + both[:, samples:]).astype(leaves.dtype)
+        if last > first:
+            part = pl.ds(first, last - first)
+            copy = pltpu.make_async_copy(leaves.at[part], leaf_out.at[part], sems.at[turn])
+            copy.start()
+            copies.append(copy)
     for height in range(1, depth + 1):
         first = 0 if height == 1 else count + 2 * (height - 2)
-        answer = solved(work[count + 2 * (height - 1)], local[height - 1])
-        level_out[0, height - 1] = sketch(work[first], work[first + 1], answer).astype(
-            level_out.dtype
-        )
+        level_out[0, height - 1] = sketch(
+            work[first], work[first + 1], answers[count + height - 1]
+        ).astype(level_out.dtype)
     for step in range(spread):
         mine = work[count + 2 * (depth - 1)] if step == 0 else tops[2 * step - 1]
         other = tops[2 * step]
@@ -441,26 +458,32 @@
         level_out[0, depth + step] = sketch(
             jnp.where(odd, other, mine), jnp.where(odd, mine, other), answer
         ).astype(level_out.dtype)
-
-
-def out_call(work, moment, local, sums, arrived, compact):
+    for copy in copies:
+        copy.wait()
+
+
+def out_call(work, answers, sums, arrived, compact):
     count, rows, samples = compact.shape
-    half = moment.shape[1]
+    half = answers.shape[1]
     spread = arrived.shape[0]
     depth = count.bit_length() - 1
     vmem = pl.BlockSpec(memory_space=pltpu.VMEM)
     return pl.pallas_call(
         out_kernel,
-        in_specs=[vmem] * 6,
-        out_specs=[vmem] * 2,
+        in_specs=[vmem] * 5,
+        out_specs=[pl.BlockSpec(memory_space=pl.ANY), vmem],
         out_shape=[
             jax.ShapeDtypeStruct((count, rows, samples), jnp.bfloat16),
             jax.ShapeDtypeStruct((1, depth + spread, samples, samples), jnp.bfloat16),
         ],
-        scratch_shapes=[pltpu.VMEM((2 * spread, half, samples), jnp.float32)],
+        scratch_shapes=[
+            pltpu.VMEM((2 * spread, half, samples), jnp.float32),
+            pltpu.VMEM((count, rows, samples), jnp.bfloat16),
+            pltpu.SemaphoreType.DMA((half // 8,)),
+        ],
         compiler_params=pltpu.CompilerParams(vmem_limit_bytes=12 * 2**20),
         name="out",
-    )(work, moment, local, sums, arrived, compact)
+    )(work, answers, sums, arrived, compact)
 
 
 def per_device(random_block, sample_block, near_blocks, near_index, near_count):
@@ -474,8 +497,8 @@
     start, moment, compact = gram_call(
         index, near_count, part, random_block, halo, held
     )
-    work, local, sums, arrived = tree_call(start, moment, spread)
-    return tuple(out_call(work, moment, local, sums, arrived, compact))
+    work, answers, sums, arrived = tree_call(start, moment, spread)
+    return tuple(out_call(work, answers, sums, arrived, compact))
 
 
 def solution(mesh):

time: 61.1 us -> 57.8 us (0.946); the launches traced: 60.6 us -> 56.7 us
  Pallas kernels: 59.9 us -> 56 us
    pallas_call x1, Pallas kernels: 8.25 us -> 5.55 us  [out_call(): pl.pallas_call(out_kernel, in_specs=[vmem] * 5, out_specs=[pl.BlockSpec(m...]
    pallas_call x1, Pallas kernels: 34.5 us -> 33.3 us  [tree_call(): pl.pallas_call(functools.partial(tree_kernel, spread), in_specs=[vmem] *...]
where the time goes in v4:
time: 57.8 us; the launch traced here: 56.7 us
  Pallas kernels  56 us (97%)
  between operations  0.7 us (1%)
    pallas_call x1, Pallas kernels, tree_call(): pl.pallas_call(functools.partial(tree_kernel, spread), in_specs=[vmem] *...  33.3 us
    pallas_call x1, Pallas kernels, halo_call(): pl.pallas_call(halo_kernel, in_specs=[fixed] * 5, out_specs=[vmem, anywhe...  14.1 us
    pallas_call x1, Pallas kernels, out_call(): pl.pallas_call(out_kernel, in_specs=[vmem] * 5, out_specs=[pl.BlockSpec(m...  5.55 us
    pallas_call x1, Pallas kernels, gram_call(): pl.pallas_call(gram_kernel, in_specs=[smem, smem, vmem, vmem, vmem, vmem]...  3.05 us

profile of v4, /device:TPU:0, one launch (start us, length us, event | category | flops | bytes accessed | tf_op | source)
XLA Modules:
  0.0 56.7 jit_solution(13029915360003551977)
XLA Ops:
  0.6 0.0 copy-start.2
  0.6 0.0 copy-start
  0.7 0.0 copy-start.1
  0.7 14.1 %halo.1 = (f32[16,256,128]{2,1,0:T(8,128)S(1)}, bf16[16,256,128]{2,1,0:T(8,128)(2,1)S(1)}, bf16[16,8,256,256]{3,2,1,0:T(8,128)(2,1)S(1)}) custom-call(s32[8,16]{1,0:T(8,128)} %bitcast.1, s32[16]{0:T(128)} %counts.1, bf16[16,256,128]{2,1,0:T(8,128)(2,1)} %source.3, bf16[16,8,256,256]{3,2,1,0:T(8,128)(2,1)} %blocks.1, bf16[16,256,128]{2,1,0:T(8,128)(2,1)} %sample.1), custom_call_target="tpu_custom_call" | custom-call | tf_op jit(solution)/shard_map/halo/pallas_call | solution.py:123
  14.7 0.0 copy-done.2
  14.8 0.0 copy-done
  14.8 0.0 copy-done.1
  14.8 3.0 %gram.1 = (f32[16,64,128]{2,1,0:T(8,128)S(1)}, f32[16,64,128]{2,1,0:T(8,128)S(1)}, bf16[16,256,128]{2,1,0:T(8,128)(2,1)S(1)}) custom-call(s32[8,16]{1,0:T(8,128)S(1)} %bitcast.2, s32[16]{0:T(128)S(1)} %copy-done.2, f32[16,256,128]{2,1,0:T(8,128)S(1)} %get-tuple-element.12.part, bf16[16,256,128]{2,1,0:T(8,128)(2,1)S(1)} %copy-done, ...), custom_call_target="tpu_custom_call" | custom-call | tf_op jit(solution)/shard_map/gram/pallas_call | solution.py:228
  17.8 33.3 %tree.1 = (f32[23,64,128]{2,1,0:T(8,128)S(1)}, f32[20,64,128]{2,1,0:T(8,128)S(1)}, f32[6,96,128]{2,1,0:T(8,128)S(1)}, f32[5,96,128]{2,1,0:T(8,128)S(1)}) custom-call(f32[16,64,128]{2,1,0:T(8,128)S(1)} %get-tuple-element.15.start, f32[16,64,128]{2,1,0:T(8,128)S(1)} %get-tuple-element.16.moment), custom_call_target="tpu_custom_call" | custom-call | tf_op jit(solution)/shard_map/tree/pallas_call | solution.py:384
  51.1 5.5 %out.1 = (bf16[16,256,128]{2,1,0:T(8,128)(2,1)}, bf16[1,9,128,128]{3,2,1,0:T(8,128)(2,1)}) custom-call(f32[23,64,128]{2,1,0:T(8,128)S(1)} %get-tuple-element.17.work, f32[20,64,128]{2,1,0:T(8,128)S(1)} %get-tuple-element.18.answers, f32[6,96,128]{2,1,0:T(8,128)S(1)} %get-tuple-element.19.sums, f32[5,96,128]{2,1,0:T(8,128)S(1)} %get-tuple-element.20.arrived, ...), custom_call_target="tpu_custom_call" | custom-call | tf_op jit(solution)/shard_map/out/pallas_call | solution.py:471
Async XLA Ops:
  0.6 14.1 %copy-start.2 = (s32[16]{0:T(128)S(1)}, s32[16]{0:T(128)}, u32[]{:S(2)}) copy-start(s32[16]{0:T(128)} %counts.1) | copy-start | bytes 196
  0.6 14.1 %copy-start = (bf16[16,256,128]{2,1,0:T(8,128)(2,1)S(1)}, bf16[16,256,128]{2,1,0:T(8,128)(2,1)}, u32[]{:S(2)}) copy-start(bf16[16,256,128]{2,1,0:T(8,128)(2,1)} %source.3) | copy-start | bytes 3145732
  0.7 14.1 %copy-start.1 = (s32[16,8]{0,1:T(8,128)S(1)}, s32[16,8]{0,1:T(8,128)}, u32[]{:S(2)}) copy-start(s32[16,8]{0,1:T(8,128)} %param.8) | copy-start | bytes 1540

commit v5 on v4

--- a/solution.py
+++ b/solution.py
@@ -325,12 +325,16 @@
     for partner in partners:
         pl.semaphore_signal(barrier, inc=1, device_id=(partner,), device_id_type=MESH)
 
-    def exchange(step):
+    chunks = sent.shape[1]
+    size = sums.shape[1] // chunks
+
+    def exchange(step, chunk):
+        part = pl.ds(chunk * size, size)
         return pltpu.make_async_remote_copy(
-            src_ref=sums.at[step],
-            dst_ref=arrived.at[step],
-            send_sem=sent.at[step],
-            recv_sem=landed.at[step],
+            src_ref=sums.at[step, part],
+            dst_ref=arrived.at[step, part],
+            send_sem=sent.at[step, chunk],
+            recv_sem=landed.at[step, chunk],
             device_id=(partners[step],),
             device_id_type=MESH,
         )
@@ -345,8 +349,8 @@
                 )
     sums[0] = packed(grams[depth, 0], moments[depth, 0])
     pl.semaphore_wait(barrier, spread)
-    copies = [exchange(step) for step in range(spread)]
-    copies[0].start()
+    for chunk in range(chunks):
+        exchange(0, chunk).start()
 
     lanes = lax.broadcasted_iota(jnp.int32, (half, samples), 1)
     diagonal = lanes - half == lax.broadcasted_iota(jnp.int32, (half, samples), 0)
@@ -369,10 +373,15 @@
         if step == spread - 1:
             for row, (node, right) in enumerate(targets):
                 answers[row] = solved(work[node], right)
-        copies[step].wait()
-        sums[step + 1] = sums[step] + arrived[step]
-        if step + 1 < spread:
-            copies[step + 1].start()
+        for chunk in range(chunks):
+            part = pl.ds(chunk * size, size)
+            exchange(step, chunk).wait_recv()
+            sums[step + 1, part] = sums[step, part] + arrived[step, part]
+            if step + 1 < spread:
+                exchange(step + 1, chunk).start()
+    for step in range(spread):
+        for chunk in range(chunks):
+            exchange(step, chunk).wait_send()
 
 
 def tree_call(start, moment, spread):
@@ -392,8 +401,8 @@
             jax.ShapeDtypeStruct((spread, rows, samples), jnp.float32),
         ],
         scratch_shapes=[
-            pltpu.SemaphoreType.DMA((spread,)),
-            pltpu.SemaphoreType.DMA((spread,)),
+            pltpu.SemaphoreType.DMA((spread, 3)),
+            pltpu.SemaphoreType.DMA((spread, 3)),
         ],
         compiler_params=pltpu.CompilerParams(
             collective_id=1, has_side_effects=True, vmem_limit_bytes=12 * 2**20

time: 57.8 us -> 57.7 us (level); the launches traced: 56.7 us -> 57.6 us
  Pallas kernels: 56 us -> 56.9 us
    pallas_call x1, Pallas kernels: 33.3 us -> 34.2 us  [tree_call(): pl.pallas_call(functools.partial(tree_kernel, spread), in_specs=[vmem] *...]
where the time goes in v5:
time: 57.7 us; the launch traced here: 57.6 us
  Pallas kernels  56.9 us (99%)
  between operations  0.7 us (1%)
    pallas_call x1, Pallas kernels, tree_call(): pl.pallas_call(functools.partial(tree_kernel, spread), in_specs=[vmem] *...  34.2 us
    pallas_call x1, Pallas kernels, halo_call(): pl.pallas_call(halo_kernel, in_specs=[fixed] * 5, out_specs=[vmem, anywhe...  14.1 us
    pallas_call x1, Pallas kernels, out_call(): pl.pallas_call(out_kernel, in_specs=[vmem] * 5, out_specs=[pl.BlockSpec(m...  5.55 us
    pallas_call x1, Pallas kernels, gram_call(): pl.pallas_call(gram_kernel, in_specs=[smem, smem, vmem, vmem, vmem, vmem]...  3.05 us

profile of v5, /device:TPU:0, one launch (start us, length us, event | category | flops | bytes accessed | tf_op | source)
XLA Modules:
  0.0 57.6 jit_solution(2810095883157559879)
XLA Ops:
  0.6 0.0 copy-start.2
  0.6 0.0 copy-start
  0.7 0.0 copy-start.1
  0.7 14.1 %halo.1 = (f32[16,256,128]{2,1,0:T(8,128)S(1)}, bf16[16,256,128]{2,1,0:T(8,128)(2,1)S(1)}, bf16[16,8,256,256]{3,2,1,0:T(8,128)(2,1)S(1)}) custom-call(s32[8,16]{1,0:T(8,128)} %bitcast.1, s32[16]{0:T(128)} %counts.1, bf16[16,256,128]{2,1,0:T(8,128)(2,1)} %source.3, bf16[16,8,256,256]{3,2,1,0:T(8,128)(2,1)} %blocks.1, bf16[16,256,128]{2,1,0:T(8,128)(2,1)} %sample.1), custom_call_target="tpu_custom_call" | custom-call | tf_op jit(solution)/shard_map/halo/pallas_call | solution.py:123
  14.7 0.0 copy-done.2
  14.8 0.0 copy-done
  14.8 0.0 copy-done.1
  14.8 3.0 %gram.1 = (f32[16,64,128]{2,1,0:T(8,128)S(1)}, f32[16,64,128]{2,1,0:T(8,128)S(1)}, bf16[16,256,128]{2,1,0:T(8,128)(2,1)S(1)}) custom-call(s32[8,16]{1,0:T(8,128)S(1)} %bitcast.2, s32[16]{0:T(128)S(1)} %copy-done.2, f32[16,256,128]{2,1,0:T(8,128)S(1)} %get-tuple-element.12.part, bf16[16,256,128]{2,1,0:T(8,128)(2,1)S(1)} %copy-done, ...), custom_call_target="tpu_custom_call" | custom-call | tf_op jit(solution)/shard_map/gram/pallas_call | solution.py:228
  17.8 34.2 %tree.1 = (f32[23,64,128]{2,1,0:T(8,128)S(1)}, f32[20,64,128]{2,1,0:T(8,128)S(1)}, f32[6,96,128]{2,1,0:T(8,128)S(1)}, f32[5,96,128]{2,1,0:T(8,128)S(1)}) custom-call(f32[16,64,128]{2,1,0:T(8,128)S(1)} %get-tuple-element.15.start, f32[16,64,128]{2,1,0:T(8,128)S(1)} %get-tuple-element.16.moment), custom_call_target="tpu_custom_call" | custom-call | tf_op jit(solution)/shard_map/tree/pallas_call | solution.py:393
  52.1 5.6 %out.1 = (bf16[16,256,128]{2,1,0:T(8,128)(2,1)}, bf16[1,9,128,128]{3,2,1,0:T(8,128)(2,1)}) custom-call(f32[23,64,128]{2,1,0:T(8,128)S(1)} %get-tuple-element.17.work, f32[20,64,128]{2,1,0:T(8,128)S(1)} %get-tuple-element.18.answers, f32[6,96,128]{2,1,0:T(8,128)S(1)} %get-tuple-element.19.sums, f32[5,96,128]{2,1,0:T(8,128)S(1)} %get-tuple-element.20.arrived, ...), custom_call_target="tpu_custom_call" | custom-call | tf_op jit(solution)/shard_map/out/pallas_call | solution.py:480
Async XLA Ops:
  0.6 14.1 %copy-start.2 = (s32[16]{0:T(128)S(1)}, s32[16]{0:T(128)}, u32[]{:S(2)}) copy-start(s32[16]{0:T(128)} %counts.1) | copy-start | bytes 196
  0.6 14.1 %copy-start = (bf16[16,256,128]{2,1,0:T(8,128)(2,1)S(1)}, bf16[16,256,128]{2,1,0:T(8,128)(2,1)}, u32[]{:S(2)}) copy-start(bf16[16,256,128]{2,1,0:T(8,128)(2,1)} %source.3) | copy-start | bytes 3145732
  0.7 14.1 %copy-start.1 = (s32[16,8]{0,1:T(8,128)S(1)}, s32[16,8]{0,1:T(8,128)}, u32[]{:S(2)}) copy-start(s32[16,8]{0,1:T(8,128)} %param.8) | copy-start | bytes 1540

commit v6 on v5

--- a/solution.py
+++ b/solution.py
@@ -366,12 +366,16 @@
             )
             place += 1
     octets = half // 8
-    turns = max(spread - 1, 1)
+    turns = max(spread - 2, 1)
+    begin = min(turns, spread - 1)
     for step in range(spread):
         if step < turns:
             factor(work, place, octets * step // turns, octets * (step + 1) // turns, 4)
-        if step == spread - 1:
-            for row, (node, right) in enumerate(targets):
+        if step >= begin:
+            some = len(targets) * (step - begin) // (spread - begin)
+            more = len(targets) * (step - begin + 1) // (spread - begin)
+            for row in range(some, more):
+                node, right = targets[row]
                 answers[row] = solved(work[node], right)
         for chunk in range(chunks):
             part = pl.ds(chunk * size, size)

time: 57.7 us -> 55.4 us (0.960)
  Pallas kernels: 56.9 us -> 54.8 us
    pallas_call x1, Pallas kernels: 34.2 us -> 32.2 us  [tree_call(): pl.pallas_call(functools.partial(tree_kernel, spread), in_specs=[vmem] *...]
where the time goes in v6:
time: 55.4 us; the launch traced here: 55.6 us
  Pallas kernels  54.8 us (99%)
  between operations  0.7 us (1%)
    pallas_call x1, Pallas kernels, tree_call(): pl.pallas_call(functools.partial(tree_kernel, spread), in_specs=[vmem] *...  32.2 us
    pallas_call x1, Pallas kernels, halo_call(): pl.pallas_call(halo_kernel, in_specs=[fixed] * 5, out_specs=[vmem, anywhe...  14.1 us
    pallas_call x1, Pallas kernels, out_call(): pl.pallas_call(out_kernel, in_specs=[vmem] * 5, out_specs=[pl.BlockSpec(m...  5.55 us
    pallas_call x1, Pallas kernels, gram_call(): pl.pallas_call(gram_kernel, in_specs=[smem, smem, vmem, vmem, vmem, vmem]...  3.05 us

profile of v6, /device:TPU:0, one launch (start us, length us, event | category | flops | bytes accessed | tf_op | source)
XLA Modules:
  0.0 55.6 jit_solution(2081826263776436810)
XLA Ops:
  0.6 0.0 copy-start.2
  0.6 0.0 copy-start
  0.7 0.0 copy-start.1
  0.7 14.1 %halo.1 = (f32[16,256,128]{2,1,0:T(8,128)S(1)}, bf16[16,256,128]{2,1,0:T(8,128)(2,1)S(1)}, bf16[16,8,256,256]{3,2,1,0:T(8,128)(2,1)S(1)}) custom-call(s32[8,16]{1,0:T(8,128)} %bitcast.1, s32[16]{0:T(128)} %counts.1, bf16[16,256,128]{2,1,0:T(8,128)(2,1)} %source.3, bf16[16,8,256,256]{3,2,1,0:T(8,128)(2,1)} %blocks.1, bf16[16,256,128]{2,1,0:T(8,128)(2,1)} %sample.1), custom_call_target="tpu_custom_call" | custom-call | tf_op jit(solution)/shard_map/halo/pallas_call | solution.py:123
  14.7 0.0 copy-done.2
  14.8 0.0 copy-done
  14.8 0.0 copy-done.1
  14.8 3.0 %gram.1 = (f32[16,64,128]{2,1,0:T(8,128)S(1)}, f32[16,64,128]{2,1,0:T(8,128)S(1)}, bf16[16,256,128]{2,1,0:T(8,128)(2,1)S(1)}) custom-call(s32[8,16]{1,0:T(8,128)S(1)} %bitcast.2, s32[16]{0:T(128)S(1)} %copy-done.2, f32[16,256,128]{2,1,0:T(8,128)S(1)} %get-tuple-element.12.part, bf16[16,256,128]{2,1,0:T(8,128)(2,1)S(1)} %copy-done, ...), custom_call_target="tpu_custom_call" | custom-call | tf_op jit(solution)/shard_map/gram/pallas_call | solution.py:228
  17.8 32.2 %tree.1 = (f32[23,64,128]{2,1,0:T(8,128)S(1)}, f32[20,64,128]{2,1,0:T(8,128)S(1)}, f32[6,96,128]{2,1,0:T(8,128)S(1)}, f32[5,96,128]{2,1,0:T(8,128)S(1)}) custom-call(f32[16,64,128]{2,1,0:T(8,128)S(1)} %get-tuple-element.15.start, f32[16,64,128]{2,1,0:T(8,128)S(1)} %get-tuple-element.16.moment), custom_call_target="tpu_custom_call" | custom-call | tf_op jit(solution)/shard_map/tree/pallas_call | solution.py:397
  50.0 5.6 %out.1 = (bf16[16,256,128]{2,1,0:T(8,128)(2,1)}, bf16[1,9,128,128]{3,2,1,0:T(8,128)(2,1)}) custom-call(f32[23,64,128]{2,1,0:T(8,128)S(1)} %get-tuple-element.17.work, f32[20,64,128]{2,1,0:T(8,128)S(1)} %get-tuple-element.18.answers, f32[6,96,128]{2,1,0:T(8,128)S(1)} %get-tuple-element.19.sums, f32[5,96,128]{2,1,0:T(8,128)S(1)} %get-tuple-element.20.arrived, ...), custom_call_target="tpu_custom_call" | custom-call | tf_op jit(solution)/shard_map/out/pallas_call | solution.py:484
Async XLA Ops:
  0.6 14.1 %copy-start.2 = (s32[16]{0:T(128)S(1)}, s32[16]{0:T(128)}, u32[]{:S(2)}) copy-start(s32[16]{0:T(128)} %counts.1) | copy-start | bytes 196
  0.6 14.1 %copy-start = (bf16[16,256,128]{2,1,0:T(8,128)(2,1)S(1)}, bf16[16,256,128]{2,1,0:T(8,128)(2,1)}, u32[]{:S(2)}) copy-start(bf16[16,256,128]{2,1,0:T(8,128)(2,1)} %source.3) | copy-start | bytes 3145732
  0.7 14.1 %copy-start.1 = (s32[16,8]{0,1:T(8,128)S(1)}, s32[16,8]{0,1:T(8,128)}, u32[]{:S(2)}) copy-start(s32[16,8]{0,1:T(8,128)} %param.8) | copy-start | bytes 1540

commit v7 on v6

--- a/solution.py
+++ b/solution.py
@@ -164,28 +164,20 @@
             needed = (place >= 0) & (place < count) & (slot < counts[box])
             picks[found] = (box * slots + slot) * count + place
             found = found + needed.astype(jnp.int32)
-    group = 4
+    group = 8
 
     def multiply(turn, carry):
-        terms = []
         for member in range(group):
             entry = turn * group + member
             code = picks[jnp.minimum(entry, found - 1)]
             block = lax.div(code, count)
             box = lax.div(block, slots)
             keep = (entry < found).astype(jnp.float32).astype(jnp.bfloat16)
-            terms.append(
-                (
-                    box,
-                    jnp.dot(
-                        blocks[box, lax.rem(block, slots)],
-                        halo[lax.rem(code, count)] * keep,
-                        preferred_element_type=jnp.float32,
-                    ),
-                )
+            far[box] -= jnp.dot(
+                blocks[box, lax.rem(block, slots)],
+                halo[lax.rem(code, count)] * keep,
+                preferred_element_type=jnp.float32,
             )
-        for box, term in terms:
-            far[box] -= term
         return carry
 
     lax.fori_loop(0, lax.div(found + group - 1, group), multiply, 0)

time: 55.4 us -> 55.8 us (level)
  no operation moved by 1% of the time
where the time goes in v7:
time: 55.8 us; the launch traced here: 55.6 us
  Pallas kernels  54.9 us (98%)
  between operations  0.7 us (1%)
    pallas_call x1, Pallas kernels, tree_call(): pl.pallas_call(functools.partial(tree_kernel, spread), in_specs=[vmem] *...  32.2 us
    pallas_call x1, Pallas kernels, halo_call(): pl.pallas_call(halo_kernel, in_specs=[fixed] * 5, out_specs=[vmem, anywhe...  14.1 us
    pallas_call x1, Pallas kernels, out_call(): pl.pallas_call(out_kernel, in_specs=[vmem] * 5, out_specs=[pl.BlockSpec(m...  5.55 us
    pallas_call x1, Pallas kernels, gram_call(): pl.pallas_call(gram_kernel, in_specs=[smem, smem, vmem, vmem, vmem, vmem]...  3.05 us

profile of v7, /device:TPU:0, one launch (start us, length us, event | category | flops | bytes accessed | tf_op | source)
XLA Modules:
  0.0 55.6 jit_solution(7307047084293788838)
XLA Ops:
  0.6 0.0 copy-start.2
  0.6 0.0 copy-start
  0.7 0.0 copy-start.1
  0.7 14.1 %halo.1 = (f32[16,256,128]{2,1,0:T(8,128)S(1)}, bf16[16,256,128]{2,1,0:T(8,128)(2,1)S(1)}, bf16[16,8,256,256]{3,2,1,0:T(8,128)(2,1)S(1)}) custom-call(s32[8,16]{1,0:T(8,128)} %bitcast.1, s32[16]{0:T(128)} %counts.1, bf16[16,256,128]{2,1,0:T(8,128)(2,1)} %source.3, bf16[16,8,256,256]{3,2,1,0:T(8,128)(2,1)} %blocks.1, bf16[16,256,128]{2,1,0:T(8,128)(2,1)} %sample.1), custom_call_target="tpu_custom_call" | custom-call | tf_op jit(solution)/shard_map/halo/pallas_call | solution.py:123
  14.7 0.0 copy-done.2
  14.8 0.0 copy-done
  14.8 0.0 copy-done.1
  14.8 3.0 %gram.1 = (f32[16,64,128]{2,1,0:T(8,128)S(1)}, f32[16,64,128]{2,1,0:T(8,128)S(1)}, bf16[16,256,128]{2,1,0:T(8,128)(2,1)S(1)}) custom-call(s32[8,16]{1,0:T(8,128)S(1)} %bitcast.2, s32[16]{0:T(128)S(1)} %copy-done.2, f32[16,256,128]{2,1,0:T(8,128)S(1)} %get-tuple-element.12.part, bf16[16,256,128]{2,1,0:T(8,128)(2,1)S(1)} %copy-done, ...), custom_call_target="tpu_custom_call" | custom-call | tf_op jit(solution)/shard_map/gram/pallas_call | solution.py:220
  17.8 32.2 %tree.1 = (f32[23,64,128]{2,1,0:T(8,128)S(1)}, f32[20,64,128]{2,1,0:T(8,128)S(1)}, f32[6,96,128]{2,1,0:T(8,128)S(1)}, f32[5,96,128]{2,1,0:T(8,128)S(1)}) custom-call(f32[16,64,128]{2,1,0:T(8,128)S(1)} %get-tuple-element.15.start, f32[16,64,128]{2,1,0:T(8,128)S(1)} %get-tuple-element.16.moment), custom_call_target="tpu_custom_call" | custom-call | tf_op jit(solution)/shard_map/tree/pallas_call | solution.py:389
  50.0 5.5 %out.1 = (bf16[16,256,128]{2,1,0:T(8,128)(2,1)}, bf16[1,9,128,128]{3,2,1,0:T(8,128)(2,1)}) custom-call(f32[23,64,128]{2,1,0:T(8,128)S(1)} %get-tuple-element.17.work, f32[20,64,128]{2,1,0:T(8,128)S(1)} %get-tuple-element.18.answers, f32[6,96,128]{2,1,0:T(8,128)S(1)} %get-tuple-element.19.sums, f32[5,96,128]{2,1,0:T(8,128)S(1)} %get-tuple-element.20.arrived, ...), custom_call_target="tpu_custom_call" | custom-call | tf_op jit(solution)/shard_map/out/pallas_call | solution.py:476
Async XLA Ops:
  0.6 14.1 %copy-start.2 = (s32[16]{0:T(128)S(1)}, s32[16]{0:T(128)}, u32[]{:S(2)}) copy-start(s32[16]{0:T(128)} %counts.1) | copy-start | bytes 196
  0.6 14.1 %copy-start = (bf16[16,256,128]{2,1,0:T(8,128)(2,1)S(1)}, bf16[16,256,128]{2,1,0:T(8,128)(2,1)}, u32[]{:S(2)}) copy-start(bf16[16,256,128]{2,1,0:T(8,128)(2,1)} %source.3) | copy-start | bytes 3145732
  0.7 14.1 %copy-start.1 = (s32[16,8]{0,1:T(8,128)S(1)}, s32[16,8]{0,1:T(8,128)}, u32[]{:S(2)}) copy-start(s32[16,8]{0,1:T(8,128)} %param.8) | copy-start | bytes 1540
